TPU v7x, 32 devices: a whole 2x2x4 slice. The times are simulated.
32 devices in a mesh: leaf: 8 (over z, x), rhs: 4 (over y, core).
Axes of the slice: x: 2, y: 2, z: 4, core: 2. Of those that a mesh axis runs over, the one named last changes fastest.
Arguments:
- charges: float32 [6144, 4096], P('leaf', 'rhs'), parts along dimension 1, may hold values from -6 to 6
- near_blocks: float32 [8, 3, 768, 768], P('leaf'), may hold values from -0.125 to 0.125
- neighbours: int32 [8, 2], P('leaf'), may hold values from 0 to 7, as said below
- compress: float32 [8, 768, 192], P('leaf'), may hold values from -0.21875 to 0.21875
- transfer: float32 [8, 3, 2, 192, 192], P('leaf'), may hold values from -0.3125 to 0.3125
- expand: float32 [8, 768, 192], P('leaf'), may hold values from -0.4375 to 0.4375
Outputs:
- potential: float32 [6144, 4096], P('leaf', 'rhs'), parts along dimension 1
There are 4 independent parts, one for each index of `rhs`. A program takes and returns all parts, laid end to end along the dimension named above; an argument that names none is the same for every part. Nothing has to cross between parts.
Inputs may be any that keep to these rules, and one draw needn't show every extreme that they name: `neighbours`: row i lists two different leaves, each of (i - 2), (i - 1), (i + 1), (i + 2) modulo 8; never i itself.
All inputs are finite; a program needn't handle non-finite values.
Results may differ from a plain program's by a relative error of at most 0.0001.
Values sent between devices are 32-bit elements; how exact they have to be, the bound alone decides.
No kernel may reach another device: no remote copies, remote signals or barrier semaphores. Data moves between devices by JAX's collectives and lax.ppermute only.
A program may use at most 128 MiB of HBM per device.

v0:
```python
import jax
import jax.numpy as jnp
from jax import lax
from jax.sharding import PartitionSpec as P


def partner(shard, axis, distance):
    return lax.ppermute(shard, axis, [(i, i ^ 1 << distance) for i in range(lax.axis_size(axis))])


def passed_along(value, axis, steps):
    count = lax.axis_size(axis)
    pairs = [(source, (source + steps) % count) for source in range(count)]
    return lax.ppermute(value, axis, pairs)


def pick_block(offset, pieces):
    chosen = jnp.zeros_like(pieces[1])
    for step in (-2, -1, 1, 2):
        chosen = jnp.where(offset == step, pieces[step], chosen)
    return chosen


def fine_sweep(coeffs, transfer, level_count):
    hi = lax.Precision.HIGHEST
    for level in range(level_count):
        partner_coeffs = partner(coeffs, "leaf", level)
        coeffs = jnp.dot(transfer[0, level, 0], coeffs, precision=hi) + jnp.dot(
            transfer[0, level, 1], partner_coeffs, precision=hi
        )
    return coeffs


def per_device(charges, near_blocks, neighbours, compress, transfer, expand):
    hi = lax.Precision.HIGHEST
    count = lax.axis_size("leaf")
    here = lax.axis_index("leaf")
    pieces = {}
    for step in (1, -1):
        pieces[step] = passed_along(charges, "leaf", -step)
    for step in (2, -2):
        pieces[step] = passed_along(charges, "leaf", -step)
    offsets = (neighbours[0] - here) % count
    offsets = jnp.where(offsets > count // 2, offsets - count, offsets)
    coeffs = jnp.einsum("ar,ac->rc", compress[0], charges, precision=hi)
    levels = count.bit_length() - 1
    coeffs = fine_sweep(coeffs, transfer, levels)
    near = jnp.dot(near_blocks[0, 0], charges, precision=hi)
    near = near + jnp.dot(near_blocks[0, 1], pick_block(offsets[0], pieces), precision=hi)
    near = near + jnp.dot(near_blocks[0, 2], pick_block(offsets[1], pieces), precision=hi)
    far = jnp.dot(expand[0], coeffs, precision=hi)
    return near + far


def solution(mesh):
    in_specs = (
        P("leaf", "rhs"),
        P("leaf", None, None, None),
        P("leaf", None),
        P("leaf", None, None),
        P("leaf", None, None, None, None),
        P("leaf", None, None),
    )
    out_specs = P("leaf", "rhs")
    return jax.shard_map(
        per_device, mesh=mesh, in_specs=in_specs, out_specs=out_specs, check_vma=False
    )
```

profile of v0, /device:TPU:0, one launch (start us, length us, event | category | flops | bytes accessed | tf_op | source)
XLA Modules:
  0.0 292.9 jit_solution(4368532836931197649)
XLA Ops:
  0.0 0.0 copy-start
  0.0 4.4 %fusion.33 = f32[192,1024]{1,0:T(8,128)S(1)} fusion(f32[768,1024]{1,0:T(8,128)} %param.6, f32[1,768,192]{1,2,0:T(8,128)} %param.9), kind=kOutput, calls=%fused_computation.35 | convolution fusion | flops 1811939328 | bytes 4521984 | tf_op jit(solution)/shard_map/ar,ac->rc/dot_general | solution.py:45
  4.4 0.0 copy-start.2
  4.4 3.0 %collective-permute-start.4 = (f32[192,1024]{1,0:T(8,128)S(1)}, f32[192,1024]{1,0:T(8,128)S(1)}, u32[]{:S(2)}, u32[]{:S(2)}) collective-permute-start(f32[192,1024]{1,0:T(8,128)S(1)} %fusion.33), channel_id=1, source_target_pairs={{0,4},{4,0},{8,12},{12,8},{16,20},{20,16},{24,28},{28,24},{1,5},{5... | collective-permute-start | bytes 2359304 | tf_op jit(solution)/shard_map/ppermute | solution.py:8
  7.5 3.6 %collective-permute-start = (f32[768,1024]{1,0:T(8,128)}, f32[768,1024]{1,0:T(8,128)}, u32[]{:S(2)}, u32[]{:S(2)}) collective-permute-start(f32[768,1024]{1,0:T(8,128)} %param.6), channel_id=1, source_target_pairs={{0,24},{4,28},{8,0},{12,4},{16,8},{20,12},{24,16},{28,20},{1,25},{... | collective-permute-start | bytes 9437192 | tf_op jit(solution)/shard_map/ppermute | solution.py:14
  11.1 0.4 collective-permute-start.1
  11.5 1.6 collective-permute-start.2
  13.1 0.0 collective-permute-start.3
  13.1 0.0 copy-done.1
  13.1 0.8 fusion.42
  13.9 11.9 %collective-permute-done.4 = f32[192,1024]{1,0:T(8,128)S(1)} collective-permute-done((f32[192,1024]{1,0:T(8,128)S(1)}, f32[192,1024]{1,0:T(8,128)S(1)}, u32[]{:S(2)}, u32[]{:S(2)}) %collective-permute-start.4) | collective-permute-done | bytes 786464 | tf_op jit(solution)/shard_map/ppermute | solution.py:8
  25.8 0.8 convolution_add_fusion.2
  26.7 2.2 collective-permute-start.5
  28.9 0.0 copy-done.2
  28.9 0.8 fusion.39
  29.7 200.3 %collective-permute-done.5 = f32[192,1024]{1,0:T(8,128)S(1)} collective-permute-done((f32[192,1024]{1,0:T(8,128)S(1)}, f32[192,1024]{1,0:T(8,128)S(1)}, u32[]{:S(2)}, u32[]{:S(2)}) %collective-permute-start.5) | collective-permute-done | bytes 786464 | tf_op jit(solution)/shard_map/ppermute | solution.py:8
  230.1 0.8 convolution_add_fusion.1
  230.9 2.2 collective-permute-start.6
  233.1 0.6 fusion.53
  239.1 0.0 slice-start
  239.1 10.4 %fusion.12 = f32[768,1024]{1,0:T(8,128)S(1)} fusion(f32[768,1024]{1,0:T(8,128)} %param.6, f32[1,3,768,768]{3,2,1,0:T(8,128)} %param.7), kind=kOutput, calls=%fused_computation.15 | convolution fusion | flops 7247757312 | bytes 8650752 | tf_op jit(solution)/shard_map/dot_general | solution.py:48
  249.5 0.0 slice-start.1
  249.5 1.8 fusion.36
  251.4 16.2 %collective-permute-done.6 = f32[192,1024]{1,0:T(8,128)S(1)} collective-permute-done((f32[192,1024]{1,0:T(8,128)S(1)}, f32[192,1024]{1,0:T(8,128)S(1)}, u32[]{:S(2)}, u32[]{:S(2)}) %collective-permute-start.6) | collective-permute-done | bytes 786464 | tf_op jit(solution)/shard_map/ppermute | solution.py:8
  267.6 2.0 convolution_add_fusion
  269.6 2.7 fusion.31
  272.3 0.0 collective-permute-done
  272.3 0.0 collective-permute-done.1
  272.4 0.0 collective-permute-done.2
  272.4 0.0 collective-permute-done.3
  272.4 9.7 %fusion.5 = f32[1024,768]{0,1:T(8,128)S(1)} fusion(f32[768,1024]{1,0:T(8,128)} %collective-permute-done, f32[768,1024]{1,0:T(8,128)} %collective-permute-done.1, f32[768,1024]{1,0:T(8,128)} %collective-permute-done.2, f32[768,1024]{1,0:T(8,128)} %collective-permute-done.3, f32[1,3,768,768]{3,2,1,0:T(8,128)S(1)} %bitcast.67, pred[]{:T(512)} %bitcast.5, ...), kind=kOutput, calls=%fused_computation.8 | convolution fusion | flops 7250903040 | bytes 18087940 | tf_op jit(solution)/shard_map/dot_general | solution.py:49
  282.1 10.7 %bitcast_add_fusion = f32[768,1024]{1,0:T(8,128)} fusion(f32[1024,768]{0,1:T(8,128)S(1)} %fusion.31, f32[768,1024]{1,0:T(8,128)S(1)} %fusion.12, f32[1024,768]{0,1:T(8,128)S(1)} %fusion.5, f32[1,3,768,768]{3,2,1,0:T(8,128)S(1)} %bitcast.67, f32[768,1024]{1,0:T(8,128)} %collective-permute-done, f32[768,1024]{1,0:T(8,128)} %collective-permute-done.1, ...), kind=kOutput, calls=%fused_computation | convolution fusion | flops 7253262336 | bytes 27525124 | tf_op jit(solution)/shard_map/dot_general | solution.py:50
  (6 shorter events, 0.0 us)
Async XLA Ops:
  0.0 269.6 %copy-start = (f32[1,768,192]{1,2,0:T(8,128)S(1)}, f32[1,768,192]{1,2,0:T(8,128)}, u32[]{:S(2)}) copy-start(f32[1,768,192]{1,2,0:T(8,128)} %param.11) | copy-start | bytes 1769476
  0.0 13.1 %copy-start.1 = (f32[1,3,2,192,192]{4,3,2,1,0:T(8,128)S(1)}, f32[1,3,2,192,192]{4,3,2,1,0:T(8,128)}, u32[]{:S(2)}) copy-start(f32[1,3,2,192,192]{4,3,2,1,0:T(8,128)} %param.10) | copy-start | bytes 2654212
  4.4 24.5 %copy-start.2 = (s32[1,2]{1,0:T(1,128)S(1)}, s32[1,2]{1,0:T(1,128)}, u32[]{:S(2)}) copy-start(s32[1,2]{1,0:T(1,128)} %param.8) | copy-start | bytes 28
  4.4 21.4 %collective-permute-start.4 = (f32[192,1024]{1,0:T(8,128)S(1)}, f32[192,1024]{1,0:T(8,128)S(1)}, u32[]{:S(2)}, u32[]{:S(2)}) collective-permute-start(f32[192,1024]{1,0:T(8,128)S(1)} %fusion.33), channel_id=1, source_target_pairs={{0,4},{4,0},{8,12},{12,8},{16,20},{20,16},{24,28},{28,24},{1,5},{5... | collective-permute-start | bytes 2359304 | tf_op jit(solution)/shard_map/ppermute | solution.py:8
  7.5 264.9 %collective-permute-start = (f32[768,1024]{1,0:T(8,128)}, f32[768,1024]{1,0:T(8,128)}, u32[]{:S(2)}, u32[]{:S(2)}) collective-permute-start(f32[768,1024]{1,0:T(8,128)} %param.6), channel_id=1, source_target_pairs={{0,24},{4,28},{8,0},{12,4},{16,8},{20,12},{24,16},{28,20},{1,25},{... | collective-permute-start | bytes 9437192 | tf_op jit(solution)/shard_map/ppermute | solution.py:14
  11.1 261.3 %collective-permute-start.1 = (f32[768,1024]{1,0:T(8,128)}, f32[768,1024]{1,0:T(8,128)}, u32[]{:S(2)}, u32[]{:S(2)}) collective-permute-start(f32[768,1024]{1,0:T(8,128)} %param.6), channel_id=1, source_target_pairs={{0,28},{4,0},{8,4},{12,8},{16,12},{20,16},{24,20},{28,24},{1,29},{... | collective-permute-start | bytes 9437192 | tf_op jit(solution)/shard_map/ppermute | solution.py:14
  11.5 260.9 %collective-permute-start.2 = (f32[768,1024]{1,0:T(8,128)}, f32[768,1024]{1,0:T(8,128)}, u32[]{:S(2)}, u32[]{:S(2)}) collective-permute-start(f32[768,1024]{1,0:T(8,128)} %param.6), channel_id=1, source_target_pairs={{0,4},{4,8},{8,12},{12,16},{16,20},{20,24},{24,28},{28,0},{1,5},{5... | collective-permute-start | bytes 9437192 | tf_op jit(solution)/shard_map/ppermute | solution.py:14
  13.1 259.3 %collective-permute-start.3 = (f32[768,1024]{1,0:T(8,128)}, f32[768,1024]{1,0:T(8,128)}, u32[]{:S(2)}, u32[]{:S(2)}) collective-permute-start(f32[768,1024]{1,0:T(8,128)} %param.6), channel_id=1, source_target_pairs={{0,8},{4,12},{8,16},{12,20},{16,24},{20,28},{24,0},{28,4},{1,9},{5... | collective-permute-start | bytes 9437192 | tf_op jit(solution)/shard_map/ppermute | solution.py:14
  26.7 203.4 %collective-permute-start.5 = (f32[192,1024]{1,0:T(8,128)S(1)}, f32[192,1024]{1,0:T(8,128)S(1)}, u32[]{:S(2)}, u32[]{:S(2)}) collective-permute-start(f32[192,1024]{1,0:T(8,128)S(1)} %bitcast.68), channel_id=1, source_target_pairs={{0,8},{4,12},{8,0},{12,4},{16,24},{20,28},{24,16},{28,20},{1,9},{5... | collective-permute-start | bytes 2359304 | tf_op jit(solution)/shard_map/ppermute | solution.py:8
  230.9 36.6 %collective-permute-start.6 = (f32[192,1024]{1,0:T(8,128)S(1)}, f32[192,1024]{1,0:T(8,128)S(1)}, u32[]{:S(2)}, u32[]{:S(2)}) collective-permute-start(f32[192,1024]{1,0:T(8,128)S(1)} %bitcast.69), channel_id=1, source_target_pairs={{0,16},{4,20},{8,24},{12,28},{16,0},{20,4},{24,8},{28,12},{1,17},{... | collective-permute-start | bytes 2359304 | tf_op jit(solution)/shard_map/ppermute | solution.py:8
  239.1 33.3 %slice-start = ((s8[7077888]{0:T(1024)(128)(4,1)}), s8[4194304]{0:T(1024)(128)(4,1)S(1)}, s32[]{:S(2)}) async-start(s8[7077888]{0:T(1024)(128)(4,1)} %bitcast.66), calls=%async_computation | async-start | bytes 8388608
  249.5 22.9 %slice-start.1 = ((s8[7077888]{0:T(1024)(128)(4,1)}), s8[2883584]{0:T(1024)(128)(4,1)S(1)}, s32[]{:S(2)}) async-start(s8[7077888]{0:T(1024)(128)(4,1)} %bitcast.66), calls=%async_computation.1 | async-start | bytes 5767168
where the time goes:
time: 293 us
  waiting for transfers between devices  228 us (78%)
  matrix products  45.2 us (15%)
  starting transfers between devices  13.1 us (4%)
  between operations  5.53 us (2%)
    ppermute x3, waiting for transfers between devices, partner(): lax.ppermute(shard, axis, [(i, i ^ 1 << distance) for i in range(lax.axis...  228 us
    dot_general x1, matrix products, per_device(): jnp.dot(near_blocks[0, 2], pick_block(offsets[1], pieces), precision=hi)  10.7 us
    dot_general x1, matrix products, per_device(): near = jnp.dot(near_blocks[0, 0], charges, precision=hi)  10.4 us
    dot_general x1, matrix products, per_device(): jnp.dot(near_blocks[0, 1], pick_block(offsets[0], pieces), precision=hi)  9.73 us
    ppermute x3, starting transfers between devices, partner(): lax.ppermute(shard, axis, [(i, i ^ 1 << distance) for i in range(lax.axis...  7.43 us
  transfers between devices with their start and end apart: 7, of which 3 were waited for; matrix products, arithmetic and copies ran while one was open for 7% of the time, Pallas kernels for 0%

commit v1 on v0

v1 whole, which is shorter than its diff:
```python
import jax
import jax.numpy as jnp
from jax import lax
from jax.sharding import PartitionSpec as P


HIGH = lax.Precision.HIGH


def dot(a, b):
    return jnp.dot(a, b, precision=HIGH)


def partner(value, distance):
    return lax.ppermute(value, "leaf", [(i, i ^ 1 << distance) for i in range(lax.axis_size("leaf"))])


def two_along(value, sense):
    count = lax.axis_size("leaf")
    pairs = [(i, (i + (2 if i % 2 else -2) * sense) % count) for i in range(count)]
    return lax.ppermute(value, "leaf", pairs)


def per_device(charges, near_blocks, neighbours, compress, transfer, expand):
    count = lax.axis_size("leaf")
    here = lax.axis_index("leaf")
    side = jnp.where(here % 2 == 0, 1, -1)
    levels = count.bit_length() - 1
    last = levels - 1

    offsets = (neighbours[0] - here) % count
    offsets = jnp.where(offsets > count // 2, offsets - count, offsets)

    def weight(step):
        second = jnp.where(offsets[1] == step, near_blocks[0, 2], 0.0)
        return jnp.where(offsets[0] == step, near_blocks[0, 1], second)

    def add(total, a, b):
        return lax.optimization_barrier(total + dot(a, b))

    far_side = two_along(charges, 1)
    near_side = two_along(charges, -1)
    mate = partner(charges, 0)
    relay = partner(far_side, 0)
    coeffs = jnp.einsum("ar,ac->rc", compress[0], charges, precision=HIGH)
    for level in range(levels):
        other = partner(coeffs, level)
        if level < last:
            coeffs = dot(transfer[0, level, 0], coeffs) + dot(transfer[0, level, 1], other)
    far_own = dot(expand[0], transfer[0, last, 0])
    far_other = dot(expand[0], transfer[0, last, 1])

    total = lax.optimization_barrier(dot(near_blocks[0, 0], charges))
    total = add(total, weight(2 * side), far_side)
    total = add(total, weight(side), mate)
    total = add(total, far_own, coeffs)
    total = add(total, weight(-side), relay)
    total = add(total, weight(-2 * side), near_side)
    total = add(total, far_other, other)
    return total


def solution(mesh):
    in_specs = (
        P("leaf", "rhs"),
        P("leaf", None, None, None),
        P("leaf", None),
        P("leaf", None, None),
        P("leaf", None, None, None, None),
        P("leaf", None, None),
    )
    out_specs = P("leaf", "rhs")
    return jax.shard_map(
        per_device, mesh=mesh, in_specs=in_specs, out_specs=out_specs, check_vma=False
    )
```

time: 293 us -> 223 us (0.76)
  waiting for transfers between devices: 228 us -> 161 us
  matrix products: 45.2 us -> 38.4 us
  other arithmetic: 0.01 us -> 4.93 us
    ppermute x7, waiting for transfers between devices: 228 us -> 161 us  [the longest x5 130 us: partner(): lax.ppermute(value, 'leaf', [(i, i ^ 1 << distance) for i in range(lax.ax...]
    dot_general x11 -> x14, matrix products: 45.2 us -> 38.4 us  [the longest x13 35.1 us: dot(): return jnp.dot(a, b, precision=HIGH)]
    add x0 -> x4, other arithmetic: none -> 4.92 us  [add(): return lax.optimization_barrier(total + dot(a, b))]
  transfers between devices with their start and end apart: 7 -> 7, of which waited for: 3 -> 4; matrix products, arithmetic and copies ran while one was open for 7% -> 17% of each run, Pallas kernels for 0% -> 0%
where the time goes in v1:
time: 223 us
  waiting for transfers between devices  161 us (72%)
  matrix products  38.4 us (17%)
  starting transfers between devices  11.8 us (5%)
  between operations  5.58 us (3%)
  other arithmetic  4.93 us (2%)
    ppermute x5, waiting for transfers between devices, partner(): lax.ppermute(value, 'leaf', [(i, i ^ 1 << distance) for i in range(lax.ax...  130 us
    dot_general x13, matrix products, dot(): return jnp.dot(a, b, precision=HIGH)  35.1 us
    ppermute x2, waiting for transfers between devices, two_along(): return lax.ppermute(value, 'leaf', pairs)  31.9 us
    ppermute x5, starting transfers between devices, partner(): lax.ppermute(value, 'leaf', [(i, i ^ 1 << distance) for i in range(lax.ax...  6.71 us
    ppermute x2, starting transfers between devices, two_along(): return lax.ppermute(value, 'leaf', pairs)  5.14 us
    add x4, other arithmetic, add(): return lax.optimization_barrier(total + dot(a, b))  4.92 us
  transfers between devices with their start and end apart: 7, of which 4 were waited for; matrix products, arithmetic and copies ran while one was open for 17% of the time, Pallas kernels for 0%

profile of v1, /device:TPU:0, one launch (start us, length us, event | category | flops | bytes accessed | tf_op | source)
XLA Modules:
  0.0 222.9 jit_solution(12527382900569866816)
XLA Ops:
  0.0 5.1 %collective-permute-start = (f32[768,1024]{1,0:T(8,128)}, f32[768,1024]{1,0:T(8,128)}, u32[]{:S(2)}, u32[]{:S(2)}) collective-permute-start(f32[768,1024]{1,0:T(8,128)} %param.6), channel_id=1, source_target_pairs={{0,24},{4,12},{8,0},{12,20},{16,8},{20,28},{24,16},{28,4},{1,25},{... | collective-permute-start | bytes 9437192 | tf_op jit(solution)/shard_map/ppermute | solution.py:21
  5.1 3.3 %fusion.45 = f32[192,1024]{1,0:T(8,128)S(1)} fusion(f32[768,1024]{1,0:T(8,128)} %param.6, f32[1,768,192]{1,2,0:T(8,128)} %param.9), kind=kOutput, calls=%fused_computation.43 | convolution fusion | flops 905969664 | bytes 4521984 | tf_op jit(solution)/shard_map/ar,ac->rc/dot_general | solution.py:45
  8.5 0.1 collective-permute-start.2
  8.6 2.0 collective-permute-start.1
  10.6 0.0 collective-permute-start.5
  10.6 0.5 fusion.56
  11.1 17.9 %collective-permute-done.2 = f32[192,1024]{1,0:T(8,128)S(1)} collective-permute-done((f32[192,1024]{1,0:T(8,128)S(1)}, f32[192,1024]{1,0:T(8,128)S(1)}, u32[]{:S(2)}, u32[]{:S(2)}) %collective-permute-start.2) | collective-permute-done | bytes 786464 | tf_op jit(solution)/shard_map/ppermute | solution.py:15
  29.0 0.5 convolution_add_fusion.1
  29.5 0.1 collective-permute-start.3
  29.5 0.7 fusion.70
  35.6 6.6 %fusion.8 = f32[768,1024]{1,0:T(8,128)S(1)} fusion(f32[768,1024]{1,0:T(8,128)} %param.6, f32[1,3,768,768]{3,2,1,0:T(8,128)} %param.7), kind=kOutput, calls=%fused_computation.8 | convolution fusion | flops 3623878656 | bytes 8650752 | tf_op jit(solution)/shard_map/dot_general | solution.py:11
  42.1 31.9 %collective-permute-done = f32[768,1024]{1,0:T(8,128)} collective-permute-done((f32[768,1024]{1,0:T(8,128)}, f32[768,1024]{1,0:T(8,128)}, u32[]{:S(2)}, u32[]{:S(2)}) %collective-permute-start) | collective-permute-done | bytes 3145760 | tf_op jit(solution)/shard_map/ppermute | solution.py:21
  74.0 2.2 collective-permute-start.4
  76.2 0.5 fusion.53
  76.7 80.4 %collective-permute-done.3 = f32[192,1024]{1,0:T(8,128)S(1)} collective-permute-done((f32[192,1024]{1,0:T(8,128)S(1)}, f32[192,1024]{1,0:T(8,128)S(1)}, u32[]{:S(2)}, u32[]{:S(2)}) %collective-permute-start.3) | collective-permute-done | bytes 786464 | tf_op jit(solution)/shard_map/ppermute | solution.py:15
  157.0 0.5 convolution_add_fusion
  157.5 2.4 %collective-permute-start.6 = (f32[192,1024]{1,0:T(8,128)S(1)}, f32[192,1024]{1,0:T(8,128)S(1)}, u32[]{:S(2)}, u32[]{:S(2)}) collective-permute-start(f32[192,1024]{1,0:T(8,128)S(1)} %bitcast.68), channel_id=1, source_target_pairs={{0,16},{4,20},{8,24},{12,28},{16,0},{20,4},{24,8},{28,12},{1,17},{... | collective-permute-start | bytes 2359304 | tf_op jit(solution)/shard_map/ppermute | solution.py:15
  159.9 0.8 fusion.49
  160.8 0.9 fusion.47
  161.6 0.0 slice-start.1
  161.6 1.5 fusion.71
  163.1 31.4 %collective-permute-done.6 = f32[192,1024]{1,0:T(8,128)S(1)} collective-permute-done((f32[192,1024]{1,0:T(8,128)S(1)}, f32[192,1024]{1,0:T(8,128)S(1)}, u32[]{:S(2)}, u32[]{:S(2)}) %collective-permute-start.6) | collective-permute-done | bytes 786464 | tf_op jit(solution)/shard_map/ppermute | solution.py:15
  194.5 1.5 fusion.72
  196.0 6.1 %fusion.27 = f32[768,1024]{1,0:T(8,128)S(1)} fusion(f32[768,1024]{1,0:T(8,128)S(1)} %fusion.8, f32[768,1024]{1,0:T(8,128)} %collective-permute-done, f32[1,3,768,768]{3,2,1,0:T(8,128)S(1)} %bitcast.66, pred[]{:T(512)S(6)} %eq.33, pred[]{:T(512)S(6)} %eq.32), kind=kOutput, calls=%fused_computation.27 | convolution fusion | flops 3625844736 | bytes 14155778 | tf_op jit(solution)/shard_map/dot_general | solution.py:11
  202.1 5.9 %fusion.4 = f32[768,1024]{1,0:T(8,128)S(1)} fusion(f32[768,1024]{1,0:T(8,128)} %collective-permute-done.1, f32[1,3,768,768]{3,2,1,0:T(8,128)S(1)} %bitcast.66, pred[]{:T(512)S(6)} %eq.35, pred[]{:T(512)S(6)} %eq.34), kind=kOutput, calls=%fused_computation.4 | convolution fusion | flops 3625058304 | bytes 11010050 | tf_op jit(solution)/shard_map/dot_general | solution.py:11
  208.0 1.0 add.44
  208.9 1.0 add.48
  209.9 5.9 %fusion = f32[768,1024]{1,0:T(8,128)S(1)} fusion(f32[768,1024]{1,0:T(8,128)} %collective-permute-done.5, f32[1,3,768,768]{3,2,1,0:T(8,128)S(1)} %bitcast.66, pred[]{:T(512)S(6)} %eq.39, pred[]{:T(512)S(6)} %eq.38), kind=kOutput, calls=%fused_computation | convolution fusion | flops 3625058304 | bytes 11010050 | tf_op jit(solution)/shard_map/dot_general | solution.py:11
  215.8 4.1 %fusion.30 = f32[768,1024]{1,0:T(8,128)S(1)} fusion(f32[768,1024]{1,0:T(8,128)S(1)} %add.48, f32[768,1024]{1,0:T(8,128)S(1)} %collective-permute-done.4, f32[1,3,768,768]{3,2,1,0:T(8,128)S(1)} %bitcast.66, pred[]{:T(512)S(6)} %eq.37, pred[]{:T(512)S(6)} %eq.36), kind=kOutput, calls=%fused_computation.28 | convolution fusion | flops 3625844736 | bytes 14155778 | tf_op jit(solution)/shard_map/dot_general | solution.py:11
  219.9 0.0 copy-start.1
  219.9 0.7 add.50
  220.6 2.3 %add.52 = f32[768,1024]{1,0:T(8,128)} add(f32[768,1024]{1,0:T(8,128)S(1)} %add.50, f32[768,1024]{1,0:T(8,128)S(1)} %fusion.72) | non-fusion elementwise | flops 786432 | bytes 9437184 | tf_op jit(solution)/shard_map/add | solution.py:39
  (15 shorter events, 0.0 us)
Async XLA Ops:
  0.0 159.9 %copy-start = (f32[1,768,192]{1,2,0:T(8,128)S(1)}, f32[1,768,192]{1,2,0:T(8,128)}, u32[]{:S(2)}) copy-start(f32[1,768,192]{1,2,0:T(8,128)} %param.11) | copy-start | bytes 1769476
  0.0 10.6 %copy-start.3 = (s32[1,2]{1,0:T(1,128)S(1)}, s32[1,2]{1,0:T(1,128)}, u32[]{:S(2)}) copy-start(s32[1,2]{1,0:T(1,128)} %param.8) | copy-start | bytes 28
  0.0 10.6 %copy-start.2 = (f32[1,3,2,192,192]{4,3,2,1,0:T(8,128)S(1)}, f32[1,3,2,192,192]{4,3,2,1,0:T(8,128)}, u32[]{:S(2)}) copy-start(f32[1,3,2,192,192]{4,3,2,1,0:T(8,128)} %param.10) | copy-start | bytes 2654212
  0.0 74.0 %collective-permute-start = (f32[768,1024]{1,0:T(8,128)}, f32[768,1024]{1,0:T(8,128)}, u32[]{:S(2)}, u32[]{:S(2)}) collective-permute-start(f32[768,1024]{1,0:T(8,128)} %param.6), channel_id=1, source_target_pairs={{0,24},{4,12},{8,0},{12,20},{16,8},{20,28},{24,16},{28,4},{1,25},{... | collective-permute-start | bytes 9437192 | tf_op jit(solution)/shard_map/ppermute | solution.py:21
  8.5 20.5 %collective-permute-start.2 = (f32[192,1024]{1,0:T(8,128)S(1)}, f32[192,1024]{1,0:T(8,128)S(1)}, u32[]{:S(2)}, u32[]{:S(2)}) collective-permute-start(f32[192,1024]{1,0:T(8,128)S(1)} %fusion.45), channel_id=1, source_target_pairs={{0,4},{4,0},{8,12},{12,8},{16,20},{20,16},{24,28},{28,24},{1,5},{5... | collective-permute-start | bytes 2359304 | tf_op jit(solution)/shard_map/ppermute | solution.py:15
  8.6 193.5 %collective-permute-start.1 = (f32[768,1024]{1,0:T(8,128)}, f32[768,1024]{1,0:T(8,128)}, u32[]{:S(2)}, u32[]{:S(2)}) collective-permute-start(f32[768,1024]{1,0:T(8,128)} %param.6), channel_id=1, source_target_pairs={{0,4},{4,0},{8,12},{12,8},{16,20},{20,16},{24,28},{28,24},{1,5},{5... | collective-permute-start | bytes 9437192 | tf_op jit(solution)/shard_map/ppermute | solution.py:15
  10.6 199.3 %collective-permute-start.5 = (f32[768,1024]{1,0:T(8,128)}, f32[768,1024]{1,0:T(8,128)}, u32[]{:S(2)}, u32[]{:S(2)}) collective-permute-start(f32[768,1024]{1,0:T(8,128)} %param.6), channel_id=1, source_target_pairs={{0,8},{4,28},{8,16},{12,4},{16,24},{20,12},{24,0},{28,20},{1,9},{5... | collective-permute-start | bytes 9437192 | tf_op jit(solution)/shard_map/ppermute | solution.py:21
  29.5 127.6 %collective-permute-start.3 = (f32[192,1024]{1,0:T(8,128)S(1)}, f32[192,1024]{1,0:T(8,128)S(1)}, u32[]{:S(2)}, u32[]{:S(2)}) collective-permute-start(f32[192,1024]{1,0:T(8,128)S(1)} %bitcast.67), channel_id=1, source_target_pairs={{0,8},{4,12},{8,0},{12,4},{16,24},{20,28},{24,16},{28,20},{1,9},{5... | collective-permute-start | bytes 2359304 | tf_op jit(solution)/shard_map/ppermute | solution.py:15
  74.0 141.8 %collective-permute-start.4 = (f32[768,1024]{1,0:T(8,128)}, f32[768,1024]{1,0:T(8,128)S(1)}, u32[]{:S(2)}, u32[]{:S(2)}) collective-permute-start(f32[768,1024]{1,0:T(8,128)} %collective-permute-done), channel_id=1, source_target_pairs={{0,4},{4,0},{8,12},{12,8},{16,20},{20,16},{24,28},{28,24},{1,5},{5... | collective-permute-start | bytes 9437192 | tf_op jit(solution)/shard_map/ppermute | solution.py:15
  157.0 38.9 %slice-start = ((s8[7077888]{0:T(1024)(128)(4,1)}), s8[4194304]{0:T(1024)(128)(4,1)S(1)}, s32[]{:S(2)}) async-start(s8[7077888]{0:T(1024)(128)(4,1)} %bitcast.65), calls=%async_computation | async-start | bytes 8388608
  157.5 37.0 %collective-permute-start.6 = (f32[192,1024]{1,0:T(8,128)S(1)}, f32[192,1024]{1,0:T(8,128)S(1)}, u32[]{:S(2)}, u32[]{:S(2)}) collective-permute-start(f32[192,1024]{1,0:T(8,128)S(1)} %bitcast.68), channel_id=1, source_target_pairs={{0,16},{4,20},{8,24},{12,28},{16,0},{20,4},{24,8},{28,12},{1,17},{... | collective-permute-start | bytes 2359304 | tf_op jit(solution)/shard_map/ppermute | solution.py:15
  161.6 34.3 %slice-start.1 = ((s8[7077888]{0:T(1024)(128)(4,1)}), s8[2883584]{0:T(1024)(128)(4,1)S(1)}, s32[]{:S(2)}) async-start(s8[7077888]{0:T(1024)(128)(4,1)} %bitcast.65), calls=%async_computation.1 | async-start | bytes 5767168
  219.9 3.0 %copy-start.1 = (f32[1,768,192]{1,2,0:T(8,128)S(1)}, f32[1,768,192]{1,2,0:T(8,128)}, u32[]{:S(2)}) copy-start(f32[1,768,192]{1,2,0:T(8,128)} %param.11) | copy-start | bytes 1769476

commit v2 on v1

v2 whole, which is shorter than its diff:
```python
import jax
import jax.numpy as jnp
from jax import lax
from jax.experimental import pallas as pl
from jax.experimental.pallas import tpu as pltpu
from jax.sharding import PartitionSpec as P


HIGH = lax.Precision.HIGH


def dot(a, b):
    return jnp.dot(a, b, precision=HIGH)


def partner(value, distance, senders=None):
    everyone = range(lax.axis_size("leaf"))
    return lax.ppermute(value, "leaf", [(i, i ^ 1 << distance) for i in senders or everyone])


def two_along(sense, count):
    return [(i, (i + (2 if i % 2 else -2) * sense) % count) for i in range(count)]


def eighths(rows, *counts):
    edges = [rows * count // 64 * 8 for count in counts] + [rows]
    return list(zip([0] + edges, edges))


def halves(value):
    high = value.astype(jnp.bfloat16)
    return high, (value - high.astype(jnp.float32)).astype(jnp.bfloat16)


def last_terms(total_ref, w_ref, near_ref, far_ref, first_ref, second_ref, out_ref):
    result = total_ref[...]
    pairs = ((w_ref[...], near_ref[...]), (far_ref[...], first_ref[...] + second_ref[...]))
    for a, b in pairs:
        a_high, a_low = halves(a)
        b_high, b_low = halves(b)
        for left, right in ((a_high, b_low), (a_low, b_high), (a_high, b_high)):
            result = result + jnp.dot(left, right, preferred_element_type=jnp.float32)
    out_ref[...] = result


def finish(total, w, near, far, first, second):
    rows, cols = total.shape
    tile = min(cols, 256)
    strip = lambda depth: pl.BlockSpec((depth, tile), lambda j: (0, j))
    whole = lambda array: pl.BlockSpec(array.shape, lambda j: (0, 0))
    depth = w.shape[1] + far.shape[1]
    return pl.pallas_call(
        last_terms,
        grid=(cols // tile,),
        out_shape=jax.ShapeDtypeStruct(total.shape, total.dtype),
        in_specs=[
            strip(rows),
            whole(w),
            strip(near.shape[0]),
            whole(far),
            strip(first.shape[0]),
            strip(second.shape[0]),
        ],
        out_specs=strip(rows),
        cost_estimate=pl.CostEstimate(
            flops=6 * rows * cols * depth, bytes_accessed=8 * rows * cols, transcendentals=0
        ),
        compiler_params=pltpu.CompilerParams(vmem_limit_bytes=24 << 20),
    )(total, w, near, far, first, second)


def per_device(charges, near_blocks, neighbours, compress, transfer, expand):
    count = lax.axis_size("leaf")
    here = lax.axis_index("leaf")
    side = jnp.where(here % 2 == 0, 1, -1)
    levels = count.bit_length() - 1
    last = levels - 1
    middle = count // 2
    outer = [i for i in range(count) if not middle // 2 <= i < count - middle // 2]
    inner = [i for i in range(count) if middle // 2 <= i < count - middle // 2]
    is_inner = (here >= middle // 2) & (here < count - middle // 2)
    shift = two_along(-1, count)
    central = [(s, t) for s, t in shift if abs(s - t) == 2 and (s < middle) != (t < middle)]
    others = [pair for pair in shift if pair not in central]
    over_middle = (here == middle) | (here == middle - 1)
    far_cuts = eighths(charges.shape[0], 4)
    near_cuts = eighths(charges.shape[0], 2, 6)

    offsets = (neighbours[0] - here) % count
    offsets = jnp.where(offsets > count // 2, offsets - count, offsets)

    def weight(step):
        second = jnp.where(offsets[1] == step, near_blocks[0, 2], 0.0)
        return jnp.where(offsets[0] == step, near_blocks[0, 1], second)

    def move(value, pairs):
        return lax.ppermute(value, "leaf", pairs)

    def add(total, a, b):
        return lax.optimization_barrier(total + dot(a, b))

    far, near, relay = [], [], []
    coeffs = jnp.einsum("ar,ac->rc", compress[0], charges, precision=HIGH)
    later, coeffs = lax.optimization_barrier((charges, coeffs))
    for part, (low, high) in enumerate(far_cuts):
        far.append(move((later if part else charges)[low:high], two_along(1, count)))
        relay.append(partner(far[part], 0))
    low, high = near_cuts[0]
    near_central = move(later[low:high], central)
    near_others = move(later[low:high], others)
    near.append(jnp.where(over_middle, near_central, near_others))
    for part, (low, high) in enumerate(near_cuts[1:], 1):
        near.append(move(later[low:high], shift))
    mate = partner(charges, 0)
    for level in range(last):
        other = partner(coeffs, level)
        coeffs = dot(transfer[0, level, 0], coeffs) + dot(transfer[0, level, 1], other)
    from_outer = partner(coeffs, last, outer)
    from_inner = partner(coeffs, last, inner)
    ends = jnp.concatenate([transfer[0, last, 0], transfer[0, last, 1]], axis=1)
    far_own, far_other = jnp.split(dot(expand[0], ends), 2, axis=1)

    w_far, w_near, w_mate, w_relay = (weight(s) for s in (2 * side, -2 * side, side, -side))

    def add_near(total, part):
        low, high = near_cuts[part]
        return add(total, w_near[:, low:high], near[part])

    total = lax.optimization_barrier(dot(near_blocks[0, 0], charges))
    total = add(total, far_own, coeffs)
    total = add(total, w_mate, mate)
    total = add(total, w_far, jnp.concatenate(far))
    total = add_near(total, 0)
    total = add_near(total, 1)
    total = add(total, w_relay, jnp.concatenate(relay))
    low, high = near_cuts[2]
    return finish(total, w_near[:, low:high], near[2], far_other, from_outer, from_inner)


def solution(mesh):
    in_specs = (
        P("leaf", "rhs"),
        P("leaf", None, None, None),
        P("leaf", None),
        P("leaf", None, None),
        P("leaf", None, None, None, None),
        P("leaf", None, None),
    )
    out_specs = P("leaf", "rhs")
    return jax.shard_map(
        per_device, mesh=mesh, in_specs=in_specs, out_specs=out_specs, check_vma=False
    )
```

time: 223 us -> 256 us (1.15)
  starting transfers between devices: 11.8 us -> 27.3 us
  local copies, waits for them, and re-layouts: 0.69 us -> 9.28 us
  Pallas kernels: 0 us -> 4.54 us
  matrix products: 38.4 us -> 41.8 us
    ppermute x7 -> x13, starting transfers between devices: 11.8 us -> 27.3 us  [the longest x6 16.3 us: move(): return lax.ppermute(value, 'leaf', pairs)]
    slice x0 -> x4, local copies, waits for them, and re-layouts: none -> 7.63 us  [the longest x2 3.34 us: per_device(): near.append(move(later[low:high], shift))]
    pallas_call x0 -> x1, Pallas kernels: none -> 4.54 us  [finish(): pl.pallas_call(last_terms, grid=(cols // tile,), out_shape=jax.ShapeDtype...]
    select_n x0 -> x1, other arithmetic: none -> 4.24 us  [weight(): return jnp.where(offsets[0] == step, near_blocks[0, 1], second)]
    dot_general x13 -> x12, matrix products: 35.1 us -> 38.5 us  [dot(): return jnp.dot(a, b, precision=HIGH)]
    ppermute x7 -> x13, waiting for transfers between devices: 161 us -> 160 us  [the longest x7 160 us: partner(): lax.ppermute(value, 'leaf', [(i, i ^ 1 << distance) for i in senders or e...]
  transfers between devices with their start and end apart: 7 -> 13, of which waited for: 4 -> 4; matrix products, arithmetic and copies ran while one was open for 17% -> 23% of each run, Pallas kernels for 0% -> 0%
where the time goes in v2:
time: 256 us; the launch traced here: 255 us
  waiting for transfers between devices  160 us (62%)
  matrix products  41.8 us (16%)
  starting transfers between devices  27.3 us (11%)
  local copies, waits for them, and re-layouts  9.28 us (4%)
  other arithmetic  6.63 us (3%)
  between operations  5.63 us (2%)
  Pallas kernels  4.54 us (2%)
    ppermute x7, waiting for transfers between devices, partner(): lax.ppermute(value, 'leaf', [(i, i ^ 1 << distance) for i in senders or e...  160 us
    dot_general x12, matrix products, dot(): return jnp.dot(a, b, precision=HIGH)  38.5 us
    ppermute x6, starting transfers between devices, move(): return lax.ppermute(value, 'leaf', pairs)  16.3 us
    ppermute x7, starting transfers between devices, partner(): lax.ppermute(value, 'leaf', [(i, i ^ 1 << distance) for i in senders or e...  11 us
  transfers between devices with their start and end apart: 13, of which 4 were waited for; matrix products, arithmetic and copies ran while one was open for 23% of the time, Pallas kernels for 0%

profile of v2, /device:TPU:0, one launch (start us, length us, event | category | flops | bytes accessed | tf_op | source)
XLA Modules:
  0.0 255.2 jit_solution(8643177342231516673)
XLA Ops:
  0.0 3.0 %collective-permute-start.2 = (f32[768,1024]{1,0:T(8,128)}, f32[768,1024]{1,0:T(8,128)}, u32[]{:S(2)}, u32[]{:S(2)}) collective-permute-start(f32[768,1024]{1,0:T(8,128)} %param.6), channel_id=1, source_target_pairs={{0,4},{4,0},{8,12},{12,8},{16,20},{20,16},{24,28},{28,24},{1,5},{5... | collective-permute-start | bytes 9437192 | tf_op jit(solution)/shard_map/ppermute | solution.py:18
  3.0 3.3 %fusion.50 = f32[192,1024]{1,0:T(8,128)S(1)} fusion(f32[768,1024]{1,0:T(8,128)} %param.6, f32[1,768,192]{1,2,0:T(8,128)} %param.9), kind=kOutput, calls=%fused_computation.49 | convolution fusion | flops 905969664 | bytes 4521984 | tf_op jit(solution)/shard_map/ar,ac->rc/dot_general | solution.py:103
  6.3 1.3 fusion.74
  7.6 1.6 collective-permute-start.5
  9.2 6.3 %collective-permute-start.6 = (f32[192,1024]{1,0:T(8,128)}, f32[192,1024]{1,0:T(8,128)}, u32[]{:S(2)}, u32[]{:S(2)}) collective-permute-start(f32[192,1024]{1,0:T(8,128)} %get-tuple-element.10), channel_id=1, source_target_pairs={{0,8},{4,28},{12,4},{16,24},{24,0},{28,20},{1,9},{5,29},{13,5},{17... | collective-permute-start | bytes 2359304 | tf_op jit(solution)/shard_map/ppermute | solution.py:97
  15.6 2.1 fusion.75
  17.7 2.1 collective-permute-start.4
  19.8 2.8 %slice.81 = f32[384,1024]{1,0:T(8,128)} slice(f32[768,1024]{1,0:T(8,128)} %param.6), slice={[0:384], [0:1024]} | slice | bytes 3145728 | tf_op jit(solution)/shard_map/slice | solution.py:106
  24.6 4.2 %select_bitcast_fusion = f32[768,768]{1,0:T(8,128)} fusion(f32[1,3,768,768]{3,2,1,0:T(8,128)} %param.7, pred[]{:T(512)S(6)} %eq.43, pred[]{:T(512)S(6)} %eq.42), kind=kLoop, calls=%fused_computation.16 | loop fusion | flops 1179648 | bytes 7077890 | tf_op jit(solution)/shard_map/jit(_where)/select_n | solution.py:94
  28.8 7.5 %fusion.12 = f32[768,1024]{1,0:T(8,128)} fusion(f32[768,1024]{1,0:T(8,128)S(1)} %copy-done.3, f32[1,3,768,768]{3,2,1,0:T(8,128)} %param.7), kind=kOutput, calls=%fused_computation.12 | convolution fusion | flops 3623878656 | bytes 8650752 | tf_op jit(solution)/shard_map/dot_general | solution.py:13
  36.3 51.9 %collective-permute-done = f32[192,1024]{1,0:T(8,128)S(1)} collective-permute-done((f32[192,1024]{1,0:T(8,128)S(1)}, f32[192,1024]{1,0:T(8,128)S(1)}, u32[]{:S(2)}, u32[]{:S(2)}) %collective-permute-start) | collective-permute-done | bytes 786464 | tf_op jit(solution)/shard_map/ppermute | solution.py:18
  88.2 3.8 %collective-permute-start.3 = (f32[384,1024]{1,0:T(8,128)}, f32[384,1024]{1,0:T(8,128)}, u32[]{:S(2)}, u32[]{:S(2)}) collective-permute-start(f32[384,1024]{1,0:T(8,128)} %slice.81), channel_id=1, source_target_pairs={{0,24},{4,12},{8,0},{12,20},{16,8},{20,28},{24,16},{28,4},{1,25},{... | collective-permute-start | bytes 4718600 | tf_op jit(solution)/shard_map/ppermute | solution.py:97
  96.7 1.5 slice.91.w_ref
  98.7 1.4 convolution_add_fusion.2
  100.2 1.0 convolution_bitcast_fusion
  101.4 1.6 fusion.58
  103.1 3.0 %fusion.46 = f32[768,1024]{1,0:T(8,128)S(1)} fusion(f32[768,768]{1,0:T(8,128)} %select_bitcast_fusion, f32[192,1024]{1,0:T(8,128)} %collective-permute-done.5, f32[192,1024]{1,0:T(8,128)} %collective-permute-done.6, pred[]{:T(512)S(6)} %or.3), kind=kOutput, calls=%fused_computation.45 | convolution fusion | flops 906166272 | bytes 5505025 | tf_op jit(solution)/shard_map/dot_general | solution.py:13
  106.1 69.6 %collective-permute-done.1 = f32[192,1024]{1,0:T(8,128)} collective-permute-done((f32[192,1024]{1,0:T(8,128)}, f32[192,1024]{1,0:T(8,128)}, u32[]{:S(2)}, u32[]{:S(2)}) %collective-permute-start.1) | collective-permute-done | bytes 786464 | tf_op jit(solution)/shard_map/ppermute | solution.py:18
  175.7 2.5 collective-permute-start.10
  178.2 1.4 collective-permute-start.9
  180.2 1.8 convolution_add_fusion.1
  182.1 1.5 convolution_add_fusion
  183.6 4.3 %collective-permute-start.11 = (f32[192,1024]{1,0:T(8,128)S(1)}, f32[192,1024]{1,0:T(8,128)S(1)}, u32[]{:S(2)}, u32[]{:S(2)}) collective-permute-start(f32[192,1024]{1,0:T(8,128)S(1)} %bitcast.59), channel_id=1, source_target_pairs={{0,16},{4,20},{24,8},{28,12},{1,17},{5,21},{25,9},{29,13},{2,18},{... | collective-permute-start | bytes 2359304 | tf_op jit(solution)/shard_map/ppermute | solution.py:18
  187.9 4.2 %fusion.35 = f32[768,1024]{1,0:T(8,128)S(1)} fusion(f32[384,1024]{1,0:T(8,128)} %collective-permute-done.7, f32[768,768]{1,0:T(8,128)S(1)} %copy-done.5), kind=kOutput, calls=%fused_computation.34 | convolution fusion | flops 1811939328 | bytes 5898240 | tf_op jit(solution)/shard_map/dot_general | solution.py:13
  192.1 6.1 %fusion = f32[768,1024]{1,0:T(8,128)S(1)} fusion(f32[384,1024]{1,0:T(8,128)} %collective-permute-done.4, f32[384,1024]{1,0:T(8,128)} %collective-permute-done.3, f32[1,3,768,768]{3,2,1,0:T(8,128)S(1)} %bitcast.58, pred[]{:T(512)S(6)} %eq.41, pred[]{:T(512)S(6)} %eq.40), kind=kOutput, calls=%fused_computation | convolution fusion | flops 3625844736 | bytes 11010050 | tf_op jit(solution)/shard_map/dot_general | solution.py:13
  198.2 1.5 collective-permute-start.12
  199.7 5.9 %fusion.32 = f32[768,1024]{1,0:T(8,128)S(1)} fusion(f32[768,1024]{1,0:T(8,128)S(1)} %convolution_add_fusion, f32[768,1024]{1,0:T(8,128)} %collective-permute-done.2, f32[1,3,768,768]{3,2,1,0:T(8,128)S(1)} %bitcast.58, pred[]{:T(512)S(6)} %eq.39, pred[]{:T(512)S(6)} %eq.38), kind=kOutput, calls=%fused_computation.30 | convolution fusion | flops 3625844736 | bytes 14155778 | tf_op jit(solution)/shard_map/dot_general | solution.py:13
  205.6 1.0 add.48
  208.0 7.7 %collective-permute-done.9 = f32[384,1024]{1,0:T(8,128)S(1)} collective-permute-done((f32[384,1024]{1,0:T(8,128)}, f32[384,1024]{1,0:T(8,128)S(1)}, u32[]{:S(2)}, u32[]{:S(2)}) %collective-permute-start.9) | collective-permute-done | bytes 1572896 | tf_op jit(solution)/shard_map/ppermute | solution.py:18
  215.7 30.8 %collective-permute-done.8 = f32[384,1024]{1,0:T(8,128)S(1)} collective-permute-done((f32[384,1024]{1,0:T(8,128)}, f32[384,1024]{1,0:T(8,128)S(1)}, u32[]{:S(2)}, u32[]{:S(2)}) %collective-permute-start.8) | collective-permute-done | bytes 1572896 | tf_op jit(solution)/shard_map/ppermute | solution.py:18
  246.5 4.1 %fusion.27.total_ref = f32[768,1024]{1,0:T(8,128)S(1)} fusion(f32[768,1024]{1,0:T(8,128)S(1)} %add.50, f32[384,1024]{1,0:T(8,128)S(1)} %collective-permute-done.9, f32[384,1024]{1,0:T(8,128)S(1)} %collective-permute-done.8, f32[1,3,768,768]{3,2,1,0:T(8,128)S(1)} %bitcast.58, pred[]{:T(512)S(6)} %eq.47, pred[]{:T(512)S(6)} %eq.46), kind=kOutput, calls=%fused_computation.29 | convolution fusion | flops 3626631168 | bytes 14155778 | tf_op jit(solution)/shard_map/dot_general | solution.py:13
  250.6 4.5 %shard_map.64 = f32[768,1024]{1,0:T(8,128)} custom-call(f32[768,1024]{1,0:T(8,128)S(1)} %fusion.27.total_ref, f32[768,192]{1,0:T(8,128)S(1)} %slice.91.w_ref, f32[192,1024]{1,0:T(8,128)S(1)} %collective-permute-done.10.near_ref, f32[768,192]{1,0:T(8,128)S(1)} %split.9.far_ref, f32[192,1024]{1,0:T(8,128)S(1)} %collective-permute-done.11.first_ref, ...), custom_call_target="tpu_custom_call" | custom-call | flops 1811939328 | bytes 6291456 | tf_op jit(solution)/shard_map/pallas_call | solution.py:52
  (49 shorter events, 4.4 us)
Async XLA Ops:
  0.0 100.2 %copy-start = (f32[1,768,192]{1,2,0:T(8,128)S(1)}, f32[1,768,192]{1,2,0:T(8,128)}, u32[]{:S(2)}) copy-start(f32[1,768,192]{1,2,0:T(8,128)} %param.11) | copy-start | bytes 1769476
  0.0 6.3 %copy-start.2 = (f32[768,1024]{1,0:T(8,128)S(1)}, f32[768,1024]{1,0:T(8,128)}, u32[]{:S(2)}) copy-start(f32[768,1024]{1,0:T(8,128)} %param.6) | copy-start | bytes 9437188
  0.0 198.2 %collective-permute-start.2 = (f32[768,1024]{1,0:T(8,128)}, f32[768,1024]{1,0:T(8,128)}, u32[]{:S(2)}, u32[]{:S(2)}) collective-permute-start(f32[768,1024]{1,0:T(8,128)} %param.6), channel_id=1, source_target_pairs={{0,4},{4,0},{8,12},{12,8},{16,20},{20,16},{24,28},{28,24},{1,5},{5... | collective-permute-start | bytes 9437192 | tf_op jit(solution)/shard_map/ppermute | solution.py:18
  7.6 92.5 %collective-permute-start.5 = (f32[192,1024]{1,0:T(8,128)}, f32[192,1024]{1,0:T(8,128)}, u32[]{:S(2)}, u32[]{:S(2)}) collective-permute-start(f32[192,1024]{1,0:T(8,128)} %get-tuple-element.10), channel_id=1, source_target_pairs={{8,16},{20,12},{9,17},{21,13},{10,18},{22,14},{11,19},{23,15}} | collective-permute-start | bytes 2359304 | tf_op jit(solution)/shard_map/ppermute | solution.py:97
  9.2 90.9 %collective-permute-start.6 = (f32[192,1024]{1,0:T(8,128)}, f32[192,1024]{1,0:T(8,128)}, u32[]{:S(2)}, u32[]{:S(2)}) collective-permute-start(f32[192,1024]{1,0:T(8,128)} %get-tuple-element.10), channel_id=1, source_target_pairs={{0,8},{4,28},{12,4},{16,24},{24,0},{28,20},{1,9},{5,29},{13,5},{17... | collective-permute-start | bytes 2359304 | tf_op jit(solution)/shard_map/ppermute | solution.py:97
  15.5 72.7 %collective-permute-start = (f32[192,1024]{1,0:T(8,128)S(1)}, f32[192,1024]{1,0:T(8,128)S(1)}, u32[]{:S(2)}, u32[]{:S(2)}) collective-permute-start(f32[192,1024]{1,0:T(8,128)S(1)} %fusion.50), channel_id=1, source_target_pairs={{0,4},{4,0},{8,12},{12,8},{16,20},{20,16},{24,28},{28,24},{1,5},{5... | collective-permute-start | bytes 2359304 | tf_op jit(solution)/shard_map/ppermute | solution.py:18
  17.7 5.0 %copy-start.11 = (s32[1,2]{1,0:T(1,128)S(1)}, s32[1,2]{1,0:T(1,128)}, u32[]{:S(2)}) copy-start(s32[1,2]{1,0:T(1,128)} %param.8) | copy-start | bytes 28
  17.7 160.5 %collective-permute-start.4 = (f32[384,1024]{1,0:T(8,128)}, f32[384,1024]{1,0:T(8,128)}, u32[]{:S(2)}, u32[]{:S(2)}) collective-permute-start(f32[384,1024]{1,0:T(8,128)} %get-tuple-element.12), channel_id=1, source_target_pairs={{0,24},{4,12},{8,0},{12,20},{16,8},{20,28},{24,16},{28,4},{1,25},{... | collective-permute-start | bytes 4718600 | tf_op jit(solution)/shard_map/ppermute | solution.py:97
  24.6 4.3 %copy-start.3 = (f32[768,1024]{1,0:T(8,128)S(1)}, f32[768,1024]{1,0:T(8,128)}, u32[]{:S(2)}) copy-start(f32[768,1024]{1,0:T(8,128)} %param.6) | copy-start | bytes 9437188
  28.8 63.2 %copy-start.6 = (f32[1,3,2,192,192]{4,3,2,1,0:T(8,128)S(1)}, f32[1,3,2,192,192]{4,3,2,1,0:T(8,128)}, u32[]{:S(2)}) copy-start(f32[1,3,2,192,192]{4,3,2,1,0:T(8,128)} %param.10) | copy-start | bytes 2654212
  88.2 8.5 %copy-start.9 = (f32[192,1024]{1,0:T(8,128)}, f32[192,1024]{1,0:T(8,128)S(1)}, u32[]{:S(2)}) copy-start(f32[192,1024]{1,0:T(8,128)S(1)} %collective-permute-done) | copy-start | bytes 2359300
  88.2 91.5 %collective-permute-start.3 = (f32[384,1024]{1,0:T(8,128)}, f32[384,1024]{1,0:T(8,128)}, u32[]{:S(2)}, u32[]{:S(2)}) collective-permute-start(f32[384,1024]{1,0:T(8,128)} %slice.81), channel_id=1, source_target_pairs={{0,24},{4,12},{8,0},{12,20},{16,8},{20,28},{24,16},{28,4},{1,25},{... | collective-permute-start | bytes 4718600 | tf_op jit(solution)/shard_map/ppermute | solution.py:97
  96.7 2.0 copy-start.10
  98.2 2.0 copy-start.7
  100.1 83.5 %collective-permute-start.7 = (f32[384,1024]{1,0:T(8,128)}, f32[384,1024]{1,0:T(8,128)}, u32[]{:S(2)}, u32[]{:S(2)}) collective-permute-start(f32[384,1024]{1,0:T(8,128)} %get-tuple-element.11), channel_id=1, source_target_pairs={{0,8},{4,28},{8,16},{12,4},{16,24},{20,12},{24,0},{28,20},{1,9},{5... | collective-permute-start | bytes 4718600 | tf_op jit(solution)/shard_map/ppermute | solution.py:97
  100.1 75.6 %collective-permute-start.1 = (f32[192,1024]{1,0:T(8,128)}, f32[192,1024]{1,0:T(8,128)}, u32[]{:S(2)}, u32[]{:S(2)}) collective-permute-start(f32[192,1024]{1,0:T(8,128)} %bitcast.9), channel_id=1, source_target_pairs={{0,8},{4,12},{8,0},{12,4},{16,24},{20,28},{24,16},{28,20},{1,9},{5... | collective-permute-start | bytes 2359304 | tf_op jit(solution)/shard_map/ppermute | solution.py:18
  103.1 72.6 %copy-start.8 = (f32[192,1024]{1,0:T(8,128)S(1)}, f32[192,1024]{1,0:T(8,128)}, u32[]{:S(2)}) copy-start(f32[192,1024]{1,0:T(8,128)} %get-tuple-element.9) | copy-start | bytes 2359300
  103.1 79.0 %copy-start.4 = (f32[768,1024]{1,0:T(8,128)S(1)}, f32[768,1024]{1,0:T(8,128)}, u32[]{:S(2)}) copy-start(f32[768,1024]{1,0:T(8,128)} %fusion.12) | copy-start | bytes 9437188
  175.7 74.9 %collective-permute-start.10 = (f32[192,1024]{1,0:T(8,128)S(1)}, f32[192,1024]{1,0:T(8,128)S(1)}, u32[]{:S(2)}, u32[]{:S(2)}) collective-permute-start(f32[192,1024]{1,0:T(8,128)S(1)} %copy-done.8), channel_id=1, source_target_pairs={{0,8},{4,28},{8,16},{12,4},{16,24},{20,12},{24,0},{28,20},{1,9},{5... | collective-permute-start | bytes 2359304 | tf_op jit(solution)/shard_map/ppermute | solution.py:97
  178.2 37.5 %collective-permute-start.9 = (f32[384,1024]{1,0:T(8,128)}, f32[384,1024]{1,0:T(8,128)S(1)}, u32[]{:S(2)}, u32[]{:S(2)}) collective-permute-start(f32[384,1024]{1,0:T(8,128)} %collective-permute-done.4), channel_id=1, source_target_pairs={{0,4},{4,0},{8,12},{12,8},{16,20},{20,16},{24,28},{28,24},{1,5},{5... | collective-permute-start | bytes 4718600 | tf_op jit(solution)/shard_map/ppermute | solution.py:18
  179.6 66.8 %collective-permute-start.8 = (f32[384,1024]{1,0:T(8,128)}, f32[384,1024]{1,0:T(8,128)S(1)}, u32[]{:S(2)}, u32[]{:S(2)}) collective-permute-start(f32[384,1024]{1,0:T(8,128)} %collective-permute-done.3), channel_id=1, source_target_pairs={{0,4},{4,0},{8,12},{12,8},{16,20},{20,16},{24,28},{28,24},{1,5},{5... | collective-permute-start | bytes 4718600 | tf_op jit(solution)/shard_map/ppermute | solution.py:18
  180.2 11.8 %slice-start = ((s8[7077888]{0:T(1024)(128)(4,1)}), s8[4194304]{0:T(1024)(128)(4,1)S(1)}, s32[]{:S(2)}) async-start(s8[7077888]{0:T(1024)(128)(4,1)} %bitcast.57), calls=%async_computation | async-start | bytes 8388608
  182.0 5.8 %copy-start.5 = (f32[768,768]{1,0:T(8,128)S(1)}, f32[768,768]{1,0:T(8,128)}, u32[]{:S(2)}) copy-start(f32[768,768]{1,0:T(8,128)} %select_bitcast_fusion) | copy-start | bytes 7077892
  182.0 10.0 %slice-start.1 = ((s8[7077888]{0:T(1024)(128)(4,1)}), s8[2883584]{0:T(1024)(128)(4,1)S(1)}, s32[]{:S(2)}) async-start(s8[7077888]{0:T(1024)(128)(4,1)} %bitcast.57), calls=%async_computation.1 | async-start | bytes 5767168
  183.6 67.0 %collective-permute-start.11 = (f32[192,1024]{1,0:T(8,128)S(1)}, f32[192,1024]{1,0:T(8,128)S(1)}, u32[]{:S(2)}, u32[]{:S(2)}) collective-permute-start(f32[192,1024]{1,0:T(8,128)S(1)} %bitcast.59), channel_id=1, source_target_pairs={{0,16},{4,20},{24,8},{28,12},{1,17},{5,21},{25,9},{29,13},{2,18},{... | collective-permute-start | bytes 2359304 | tf_op jit(solution)/shard_map/ppermute | solution.py:18
  198.2 52.4 %collective-permute-start.12 = (f32[192,1024]{1,0:T(8,128)S(1)}, f32[192,1024]{1,0:T(8,128)S(1)}, u32[]{:S(2)}, u32[]{:S(2)}) collective-permute-start(f32[192,1024]{1,0:T(8,128)S(1)} %bitcast.60), channel_id=1, source_target_pairs={{8,24},{12,28},{16,0},{20,4},{9,25},{13,29},{17,1},{21,5},{10,26},... | collective-permute-start | bytes 2359304 | tf_op jit(solution)/shard_map/ppermute | solution.py:18
  250.6 4.6 %copy-start.1 = (f32[1,768,192]{1,2,0:T(8,128)S(1)}, f32[1,768,192]{1,2,0:T(8,128)}, u32[]{:S(2)}) copy-start(f32[1,768,192]{1,2,0:T(8,128)} %param.11) | copy-start | bytes 1769476

commit v3 on v2

--- a/solution.py
+++ b/solution.py
@@ -27,46 +27,50 @@
     return list(zip([0] + edges, edges))
 
 
-def halves(value):
-    high = value.astype(jnp.bfloat16)
-    return high, (value - high.astype(jnp.float32)).astype(jnp.bfloat16)
+def three_pass(weight):
+    high = lax.reduce_precision(weight, exponent_bits=8, mantissa_bits=7)
+    parts = [high, weight - high, high]
+    return jnp.concatenate([part.astype(jnp.bfloat16) for part in parts], axis=1)
 
 
-def last_terms(total_ref, w_ref, near_ref, far_ref, first_ref, second_ref, out_ref):
-    result = total_ref[...]
-    pairs = ((w_ref[...], near_ref[...]), (far_ref[...], first_ref[...] + second_ref[...]))
-    for a, b in pairs:
-        a_high, a_low = halves(a)
-        b_high, b_low = halves(b)
-        for left, right in ((a_high, b_low), (a_low, b_high), (a_high, b_high)):
-            result = result + jnp.dot(left, right, preferred_element_type=jnp.float32)
-    out_ref[...] = result
+def last_term(total_ref, left_ref, right_ref, out_ref, strips, sems):
+    tile = strips.shape[2]
+    copies = []
+    for part in range(strips.shape[0]):
+        columns = pl.ds(part * tile, tile)
+        value = right_ref[:, columns]
+        high = value.astype(jnp.bfloat16)
+        low = (value - high.astype(jnp.float32)).astype(jnp.bfloat16)
+        right = jnp.concatenate([high, high, low])
+        term = jnp.dot(left_ref[...], right, preferred_element_type=jnp.float32)
+        strips[part] = total_ref[:, columns] + term
+        copy = pltpu.make_async_copy(strips.at[part], out_ref.at[:, columns], sems.at[part])
+        copy.start()
+        copies.append(copy)
+    for copy in copies:
+        copy.wait()
 
 
-def finish(total, w, near, far, first, second):
+def finish(total, left, right):
     rows, cols = total.shape
     tile = min(cols, 256)
-    strip = lambda depth: pl.BlockSpec((depth, tile), lambda j: (0, j))
-    whole = lambda array: pl.BlockSpec(array.shape, lambda j: (0, 0))
-    depth = w.shape[1] + far.shape[1]
+    local = pltpu.VMEM
+    operands = [pltpu.with_memory_space_constraint(value, local) for value in (total, left, right)]
+    depth = left.shape[1]
     return pl.pallas_call(
-        last_terms,
-        grid=(cols // tile,),
+        last_term,
         out_shape=jax.ShapeDtypeStruct(total.shape, total.dtype),
-        in_specs=[
-            strip(rows),
-            whole(w),
-            strip(near.shape[0]),
-            whole(far),
-            strip(first.shape[0]),
-            strip(second.shape[0]),
+        in_specs=[pl.BlockSpec(memory_space=local)] * len(operands),
+        out_specs=pl.BlockSpec(memory_space=pl.ANY),
+        scratch_shapes=[
+            pltpu.VMEM((cols // tile, rows, tile), total.dtype),
+            pltpu.SemaphoreType.DMA((cols // tile,)),
         ],
-        out_specs=strip(rows),
         cost_estimate=pl.CostEstimate(
-            flops=6 * rows * cols * depth, bytes_accessed=8 * rows * cols, transcendentals=0
+            flops=2 * rows * cols * depth, bytes_accessed=8 * rows * cols, transcendentals=0
         ),
         compiler_params=pltpu.CompilerParams(vmem_limit_bytes=24 << 20),
-    )(total, w, near, far, first, second)
+    )(*operands)
 
 
 def per_device(charges, near_blocks, neighbours, compress, transfer, expand):
@@ -83,8 +87,7 @@
     central = [(s, t) for s, t in shift if abs(s - t) == 2 and (s < middle) != (t < middle)]
     others = [pair for pair in shift if pair not in central]
     over_middle = (here == middle) | (here == middle - 1)
-    far_cuts = eighths(charges.shape[0], 4)
-    near_cuts = eighths(charges.shape[0], 2, 6)
+    cuts = eighths(charges.shape[0], 4, 7)
 
     offsets = (neighbours[0] - here) % count
     offsets = jnp.where(offsets > count // 2, offsets - count, offsets)
@@ -102,14 +105,14 @@
     far, near, relay = [], [], []
     coeffs = jnp.einsum("ar,ac->rc", compress[0], charges, precision=HIGH)
     later, coeffs = lax.optimization_barrier((charges, coeffs))
-    for part, (low, high) in enumerate(far_cuts):
+    for part, (low, high) in enumerate(cuts):
         far.append(move((later if part else charges)[low:high], two_along(1, count)))
         relay.append(partner(far[part], 0))
-    low, high = near_cuts[0]
+    low, high = cuts[0]
     near_central = move(later[low:high], central)
     near_others = move(later[low:high], others)
     near.append(jnp.where(over_middle, near_central, near_others))
-    for part, (low, high) in enumerate(near_cuts[1:], 1):
+    for part, (low, high) in enumerate(cuts[1:], 1):
         near.append(move(later[low:high], shift))
     mate = partner(charges, 0)
     for level in range(last):
@@ -123,7 +126,7 @@
     w_far, w_near, w_mate, w_relay = (weight(s) for s in (2 * side, -2 * side, side, -side))
 
     def add_near(total, part):
-        low, high = near_cuts[part]
+        low, high = cuts[part]
         return add(total, w_near[:, low:high], near[part])
 
     total = lax.optimization_barrier(dot(near_blocks[0, 0], charges))
@@ -131,10 +134,13 @@
     total = add(total, w_mate, mate)
     total = add(total, w_far, jnp.concatenate(far))
     total = add_near(total, 0)
+    low, high = cuts[-1]
+    total = add(total, w_relay[:, :low], jnp.concatenate(relay[:-1]))
+    total = add(total, w_relay[:, low:high], relay[-1])
     total = add_near(total, 1)
-    total = add(total, w_relay, jnp.concatenate(relay))
-    low, high = near_cuts[2]
-    return finish(total, w_near[:, low:high], near[2], far_other, from_outer, from_inner)
+    total = add(total, far_other, jnp.where(is_inner, from_outer, from_inner))
+    low, high = cuts[-1]
+    return finish(total, three_pass(w_near[:, low:high]), near[-1])
 
 
 def solution(mesh):

time: 256 us -> 239 us (0.934)
  waiting for transfers between devices: 160 us -> 88.6 us
  starting transfers between devices: 27.3 us -> 73 us
  matrix products: 41.8 us -> 51.1 us
  other arithmetic: 6.63 us -> 10 us
  local copies, waits for them, and re-layouts: 9.28 us -> 6.7 us
    ppermute x7 -> x8, waiting for transfers between devices: 160 us -> 72.9 us  [partner(): lax.ppermute(value, 'leaf', [(i, i ^ 1 << distance) for i in senders or e...]
    ppermute x7 -> x8, starting transfers between devices: 11 us -> 53.5 us  [partner(): lax.ppermute(value, 'leaf', [(i, i ^ 1 << distance) for i in senders or e...]
    ppermute x6 -> x7, waiting for transfers between devices: 0.02 us -> 15.7 us  [move(): return lax.ppermute(value, 'leaf', pairs)]
    dot_general x12 -> x14, matrix products: 38.5 us -> 46.8 us  [dot(): return jnp.dot(a, b, precision=HIGH)]
    ppermute x6 -> x7, starting transfers between devices: 16.3 us -> 19.4 us  [move(): return lax.ppermute(value, 'leaf', pairs)]
  transfers between devices with their start and end apart: 13 -> 15, of which waited for: 4 -> 4; matrix products, arithmetic and copies ran while one was open for 23% -> 29% of each run, Pallas kernels for 0% -> 0%
where the time goes in v3:
time: 239 us; the launch traced here: 237 us
  waiting for transfers between devices  88.6 us (37%)
  starting transfers between devices  73 us (31%)
  matrix products  51.1 us (21%)
  other arithmetic  10 us (4%)
  local copies, waits for them, and re-layouts  6.7 us (3%)
  between operations  5.33 us (2%)
    ppermute x8, waiting for transfers between devices, partner(): lax.ppermute(value, 'leaf', [(i, i ^ 1 << distance) for i in senders or e...  72.9 us
    ppermute x8, starting transfers between devices, partner(): lax.ppermute(value, 'leaf', [(i, i ^ 1 << distance) for i in senders or e...  53.5 us
    dot_general x14, matrix products, dot(): return jnp.dot(a, b, precision=HIGH)  46.8 us
    ppermute x7, starting transfers between devices, move(): return lax.ppermute(value, 'leaf', pairs)  19.4 us
    ppermute x7, waiting for transfers between devices, move(): return lax.ppermute(value, 'leaf', pairs)  15.7 us
    add x5, other arithmetic, add(): return lax.optimization_barrier(total + dot(a, b))  4.79 us
  transfers between devices with their start and end apart: 15, of which 4 were waited for; matrix products, arithmetic and copies ran while one was open for 29% of the time, Pallas kernels for 0%

profile of v3, /device:TPU:0, one launch (start us, length us, event | category | flops | bytes accessed | tf_op | source)
XLA Modules:
  0.0 237.0 jit_solution(3807869315924937914)
XLA Ops:
  0.0 3.0 %collective-permute-start.2 = (f32[768,1024]{1,0:T(8,128)}, f32[768,1024]{1,0:T(8,128)}, u32[]{:S(2)}, u32[]{:S(2)}) collective-permute-start(f32[768,1024]{1,0:T(8,128)} %param.6), channel_id=1, source_target_pairs={{0,4},{4,0},{8,12},{12,8},{16,20},{20,16},{24,28},{28,24},{1,5},{5... | collective-permute-start | bytes 9437192 | tf_op jit(solution)/shard_map/ppermute | solution.py:18
  3.0 4.2 %fusion.49 = f32[192,1024]{1,0:T(8,128)} fusion(f32[768,1024]{1,0:T(8,128)} %param.6, f32[1,768,192]{1,2,0:T(8,128)} %param.9), kind=kOutput, calls=%fused_computation.50 | convolution fusion | flops 905969664 | bytes 4521984 | tf_op jit(solution)/shard_map/ar,ac->rc/dot_general | solution.py:106
  8.1 4.3 %collective-permute-start.5 = (f32[96,1024]{1,0:T(8,128)}, f32[96,1024]{1,0:T(8,128)}, u32[]{:S(2)}, u32[]{:S(2)}) collective-permute-start(f32[96,1024]{1,0:T(8,128)} %slice.88), channel_id=1, source_target_pairs={{0,24},{4,12},{8,0},{12,20},{16,8},{20,28},{24,16},{28,4},{1,25},{... | collective-permute-start | bytes 1179656 | tf_op jit(solution)/shard_map/ppermute | solution.py:100
  12.5 1.3 slice.86
  15.4 1.6 collective-permute-start.11
  20.0 2.8 %select_bitcast_fusion = (f32[768,768]{1,0:T(8,128)S(1)}, f32[768,768]{1,0:T(8,128)S(1)}) fusion(f32[1,3,768,768]{3,2,1,0:T(8,128)} %param.7, pred[]{:T(512)S(6)} %eq.47, pred[]{:T(512)S(6)} %eq.46, pred[]{:T(512)S(6)} %eq.43, pred[]{:T(512)S(6)} %eq.42), kind=kLoop, calls=%fused_computation.16 | loop fusion | flops 2359296 | bytes 9437188 | tf_op jit(solution)/shard_map/jit(_where)/select_n | solution.py:97
  23.9 1.6 fusion.63
  25.5 7.2 %fusion.14 = f32[768,1024]{1,0:T(8,128)} fusion(f32[768,1024]{1,0:T(8,128)S(1)} %copy-done.3, f32[1,3,768,768]{3,2,1,0:T(8,128)} %param.7), kind=kOutput, calls=%fused_computation.14 | convolution fusion | flops 3623878656 | bytes 8650752 | tf_op jit(solution)/shard_map/dot_general | solution.py:13
  32.8 55.5 %collective-permute-done = f32[192,1024]{1,0:T(8,128)} collective-permute-done((f32[192,1024]{1,0:T(8,128)}, f32[192,1024]{1,0:T(8,128)}, u32[]{:S(2)}, u32[]{:S(2)}) %collective-permute-start) | collective-permute-done | bytes 786464 | tf_op jit(solution)/shard_map/ppermute | solution.py:18
  88.3 2.5 %convolution_add_fusion.2 = f32[1024,192]{0,1:T(8,128)} fusion(f32[1024,192]{0,1:T(8,128)S(1)} %fusion.63, f32[192,1024]{1,0:T(8,128)} %collective-permute-done, f32[1,3,2,192,192]{4,3,2,1,0:T(8,128)S(1)} %copy-done.8), kind=kOutput, calls=%fused_computation.34 | convolution fusion | flops 226689024 | bytes 2555904 | tf_op jit(solution)/shard_map/dot_general | solution.py:13
  90.8 1.8 collective-permute-start.1
  95.0 2.7 %slice.90 = f32[384,1024]{1,0:T(8,128)} slice(f32[768,1024]{1,0:T(8,128)} %param.6), slice={[0:384], [0:1024]} | slice | bytes 3145728 | tf_op jit(solution)/shard_map/slice | solution.py:112
  97.8 1.5 collective-permute-start.10
  101.4 6.3 %collective-permute-done.10 = f32[96,1024]{1,0:T(8,128)S(1)} collective-permute-done((f32[96,1024]{1,0:T(8,128)}, f32[96,1024]{1,0:T(8,128)S(1)}, u32[]{:S(2)}, u32[]{:S(2)}) %collective-permute-start.10) | collective-permute-done | bytes 393248 | tf_op jit(solution)/shard_map/ppermute | solution.py:18
  108.5 1.5 fusion.53
  110.0 2.5 %collective-permute-start.4 = (f32[288,1024]{1,0:T(8,128)}, f32[288,1024]{1,0:T(8,128)}, u32[]{:S(2)}, u32[]{:S(2)}) collective-permute-start(f32[288,1024]{1,0:T(8,128)} %slice.87), channel_id=1, source_target_pairs={{0,24},{4,12},{8,0},{12,20},{16,8},{20,28},{24,16},{28,4},{1,25},{... | collective-permute-start | bytes 3538952 | tf_op jit(solution)/shard_map/ppermute | solution.py:100
  112.5 4.2 %collective-permute-start.7 = (f32[384,1024]{1,0:T(8,128)S(1)}, f32[384,1024]{1,0:T(8,128)}, u32[]{:S(2)}, u32[]{:S(2)}) collective-permute-start(f32[384,1024]{1,0:T(8,128)S(1)} %copy-done.7), channel_id=1, source_target_pairs={{0,8},{4,28},{12,4},{16,24},{24,0},{28,20},{1,9},{5,29},{13,5},{17... | collective-permute-start | bytes 4718600 | tf_op jit(solution)/shard_map/ppermute | solution.py:100
  116.7 1.6 fusion.60
  118.4 4.1 %fusion.35 = f32[768,1024]{1,0:T(8,128)S(1)} fusion(f32[288,1024]{1,0:T(8,128)} %collective-permute-done.11, f32[768,768]{1,0:T(8,128)S(1)} %copy-done.6), kind=kOutput, calls=%fused_computation.35 | convolution fusion | flops 1358954496 | bytes 5505024 | tf_op jit(solution)/shard_map/dot_general | solution.py:13
  122.5 1.6 convolution_add_fusion.1
  124.2 1.5 convolution_add_fusion
  125.7 15.7 %collective-permute-done.4 = f32[288,1024]{1,0:T(8,128)} collective-permute-done((f32[288,1024]{1,0:T(8,128)}, f32[288,1024]{1,0:T(8,128)}, u32[]{:S(2)}, u32[]{:S(2)}) %collective-permute-start.4) | collective-permute-done | bytes 1179680 | tf_op jit(solution)/shard_map/ppermute | solution.py:100
  141.4 43.7 %collective-permute-start.12 = (f32[192,1024]{1,0:T(8,128)S(1)}, f32[192,1024]{1,0:T(8,128)}, u32[]{:S(2)}, u32[]{:S(2)}) collective-permute-start(f32[192,1024]{1,0:T(8,128)S(1)} %bitcast.57), channel_id=1, source_target_pairs={{0,16},{4,20},{24,8},{28,12},{1,17},{5,21},{25,9},{29,13},{2,18},{... | collective-permute-start | bytes 2359304 | tf_op jit(solution)/shard_map/ppermute | solution.py:18
  186.4 2.0 collective-permute-start.8
  188.4 6.2 %fusion = f32[768,1024]{1,0:T(8,128)S(1)} fusion(f32[96,1024]{1,0:T(8,128)} %collective-permute-done.5, f32[288,1024]{1,0:T(8,128)} %collective-permute-done.4, f32[384,1024]{1,0:T(8,128)} %collective-permute-done.3, f32[1,3,768,768]{3,2,1,0:T(8,128)S(1)} %bitcast.56, pred[]{:T(512)S(6)} %eq.41, pred[]{:T(512)S(6)} %eq.40), kind=kOutput, calls=%fused_computation | convolution fusion | flops 3626631168 | bytes 11010050 | tf_op jit(solution)/shard_map/dot_general | solution.py:13
  194.7 4.1 %fusion.33 = f32[768,1024]{1,0:T(8,128)S(1)} fusion(f32[384,1024]{1,0:T(8,128)S(1)} %collective-permute-done.6, f32[384,1024]{1,0:T(8,128)} %collective-permute-done.7, f32[768,768]{1,0:T(8,128)S(1)} %copy-done.6, pred[]{:T(512)S(6)} %or.3), kind=kOutput, calls=%fused_computation.30 | convolution fusion | flops 1812332544 | bytes 7471105 | tf_op jit(solution)/shard_map/dot_general | solution.py:13
  198.9 5.7 %collective-permute-start.14 = (f32[96,1024]{1,0:T(8,128)}, f32[96,1024]{1,0:T(8,128)S(1)}, u32[]{:S(2)}, u32[]{:S(2)}) collective-permute-start(f32[96,1024]{1,0:T(8,128)} %slice.88), channel_id=1, source_target_pairs={{0,8},{4,28},{8,16},{12,4},{16,24},{20,12},{24,0},{28,20},{1,9},{5... | collective-permute-start | bytes 1179656 | tf_op jit(solution)/shard_map/ppermute | solution.py:100
  204.5 11.0 %collective-permute-done.13 = f32[192,1024]{1,0:T(8,128)} collective-permute-done((f32[192,1024]{1,0:T(8,128)S(1)}, f32[192,1024]{1,0:T(8,128)}, u32[]{:S(2)}, u32[]{:S(2)}) %collective-permute-start.13) | collective-permute-done | bytes 786464 | tf_op jit(solution)/shard_map/ppermute | solution.py:18
  215.6 2.6 %fusion.44 = f32[768,1024]{1,0:T(8,128)S(1)} fusion(f32[192,1024]{1,0:T(8,128)} %collective-permute-done.12, f32[192,1024]{1,0:T(8,128)} %collective-permute-done.13, f32[768,384]{0,1:T(8,128)S(1)} %convolution_bitcast_fusion, pred[]{:T(512)S(6)} %and.16), kind=kOutput, calls=%fused_computation.44 | convolution fusion | flops 906166272 | bytes 5308417 | tf_op jit(solution)/shard_map/dot_general | solution.py:13
  218.2 5.9 %fusion.30 = f32[768,1024]{1,0:T(8,128)S(1)} fusion(f32[768,1024]{1,0:T(8,128)S(1)} %convolution_add_fusion, f32[768,1024]{1,0:T(8,128)} %collective-permute-done.2, f32[1,3,768,768]{3,2,1,0:T(8,128)S(1)} %bitcast.56, pred[]{:T(512)S(6)} %eq.39, pred[]{:T(512)S(6)} %eq.38), kind=kOutput, calls=%fused_computation.29 | convolution fusion | flops 3625844736 | bytes 14155778 | tf_op jit(solution)/shard_map/dot_general | solution.py:13
  226.1 5.4 %fusion.25 = f32[768,1024]{1,0:T(8,128)S(1)} fusion(f32[768,1024]{1,0:T(8,128)S(1)} %add.55, f32[288,1024]{1,0:T(8,128)S(1)} %collective-permute-done.9, f32[384,1024]{1,0:T(8,128)} %collective-permute-done.8, f32[768,768]{1,0:T(8,128)S(1)} %get-tuple-element.9), kind=kOutput, calls=%fused_computation.28 | convolution fusion | flops 3172368384 | bytes 11403264 | tf_op jit(solution)/shard_map/dot_general | solution.py:13
  234.4 2.3 shard_map.64
  (54 shorter events, 13.3 us)
Async XLA Ops:
  0.0 100.6 %copy-start = (f32[1,768,192]{1,2,0:T(8,128)S(1)}, f32[1,768,192]{1,2,0:T(8,128)}, u32[]{:S(2)}) copy-start(f32[1,768,192]{1,2,0:T(8,128)} %param.11) | copy-start | bytes 1769476
  0.0 7.4 %copy-start.2 = (f32[768,1024]{1,0:T(8,128)S(1)}, f32[768,1024]{1,0:T(8,128)}, u32[]{:S(2)}) copy-start(f32[768,1024]{1,0:T(8,128)} %param.6) | copy-start | bytes 9437188
  0.0 218.2 %collective-permute-start.2 = (f32[768,1024]{1,0:T(8,128)}, f32[768,1024]{1,0:T(8,128)}, u32[]{:S(2)}, u32[]{:S(2)}) collective-permute-start(f32[768,1024]{1,0:T(8,128)} %param.6), channel_id=1, source_target_pairs={{0,4},{4,0},{8,12},{12,8},{16,20},{20,16},{24,28},{28,24},{1,5},{5... | collective-permute-start | bytes 9437192 | tf_op jit(solution)/shard_map/ppermute | solution.py:18
  7.2 81.1 %collective-permute-start = (f32[192,1024]{1,0:T(8,128)}, f32[192,1024]{1,0:T(8,128)}, u32[]{:S(2)}, u32[]{:S(2)}) collective-permute-start(f32[192,1024]{1,0:T(8,128)} %fusion.49), channel_id=1, source_target_pairs={{0,4},{4,0},{8,12},{12,8},{16,20},{20,16},{24,28},{28,24},{1,5},{5... | collective-permute-start | bytes 2359304 | tf_op jit(solution)/shard_map/ppermute | solution.py:18
  8.1 8.8 %copy-start.9 = (s32[1,2]{1,0:T(1,128)S(1)}, s32[1,2]{1,0:T(1,128)}, u32[]{:S(2)}) copy-start(s32[1,2]{1,0:T(1,128)} %param.8) | copy-start | bytes 28
  8.1 89.6 %collective-permute-start.5 = (f32[96,1024]{1,0:T(8,128)}, f32[96,1024]{1,0:T(8,128)}, u32[]{:S(2)}, u32[]{:S(2)}) collective-permute-start(f32[96,1024]{1,0:T(8,128)} %slice.88), channel_id=1, source_target_pairs={{0,24},{4,12},{8,0},{12,20},{16,8},{20,28},{24,16},{28,4},{1,25},{... | collective-permute-start | bytes 1179656 | tf_op jit(solution)/shard_map/ppermute | solution.py:100
  13.8 171.3 %collective-permute-start.3 = (f32[384,1024]{1,0:T(8,128)}, f32[384,1024]{1,0:T(8,128)}, u32[]{:S(2)}, u32[]{:S(2)}) collective-permute-start(f32[384,1024]{1,0:T(8,128)} %slice.86), channel_id=1, source_target_pairs={{0,24},{4,12},{8,0},{12,20},{16,8},{20,28},{24,16},{28,4},{1,25},{... | collective-permute-start | bytes 4718600 | tf_op jit(solution)/shard_map/ppermute | solution.py:100
  15.4 94.6 %collective-permute-start.11 = (f32[288,1024]{1,0:T(8,128)}, f32[288,1024]{1,0:T(8,128)}, u32[]{:S(2)}, u32[]{:S(2)}) collective-permute-start(f32[288,1024]{1,0:T(8,128)} %slice.87), channel_id=1, source_target_pairs={{0,8},{4,28},{8,16},{12,4},{16,24},{20,12},{24,0},{28,20},{1,9},{5... | collective-permute-start | bytes 3538952 | tf_op jit(solution)/shard_map/ppermute | solution.py:100
  20.0 3.9 %copy-start.8 = (f32[1,3,2,192,192]{4,3,2,1,0:T(8,128)S(1)}, f32[1,3,2,192,192]{4,3,2,1,0:T(8,128)}, u32[]{:S(2)}) copy-start(f32[1,3,2,192,192]{4,3,2,1,0:T(8,128)} %param.10) | copy-start | bytes 2654212
  20.0 5.5 %copy-start.3 = (f32[768,1024]{1,0:T(8,128)S(1)}, f32[768,1024]{1,0:T(8,128)}, u32[]{:S(2)}) copy-start(f32[768,1024]{1,0:T(8,128)} %param.6) | copy-start | bytes 9437188
  22.9 9.9 %copy-start.5 = (f32[768,768]{1,0:T(8,128)}, f32[768,768]{1,0:T(8,128)S(1)}, u32[]{:S(2)}) copy-start(f32[768,768]{1,0:T(8,128)S(1)} %get-tuple-element.10) | copy-start | bytes 7077892
  90.8 21.7 %collective-permute-start.1 = (f32[192,1024]{1,0:T(8,128)}, f32[192,1024]{1,0:T(8,128)}, u32[]{:S(2)}, u32[]{:S(2)}) collective-permute-start(f32[192,1024]{1,0:T(8,128)} %bitcast.9), channel_id=1, source_target_pairs={{0,8},{4,12},{8,0},{12,4},{16,24},{20,28},{24,16},{28,20},{1,9},{5... | collective-permute-start | bytes 2359304 | tf_op jit(solution)/shard_map/ppermute | solution.py:18
  97.8 9.9 %copy-start.7 = (f32[384,1024]{1,0:T(8,128)S(1)}, f32[384,1024]{1,0:T(8,128)}, u32[]{:S(2)}) copy-start(f32[384,1024]{1,0:T(8,128)} %slice.90) | copy-start | bytes 4718596
  97.8 9.9 %collective-permute-start.10 = (f32[96,1024]{1,0:T(8,128)}, f32[96,1024]{1,0:T(8,128)S(1)}, u32[]{:S(2)}, u32[]{:S(2)}) collective-permute-start(f32[96,1024]{1,0:T(8,128)} %collective-permute-done.5), channel_id=1, source_target_pairs={{0,4},{4,0},{8,12},{12,8},{16,20},{20,16},{24,28},{28,24},{1,5},{5... | collective-permute-start | bytes 1179656 | tf_op jit(solution)/shard_map/ppermute | solution.py:18
  107.7 78.7 %collective-permute-start.6 = (f32[384,1024]{1,0:T(8,128)S(1)}, f32[384,1024]{1,0:T(8,128)S(1)}, u32[]{:S(2)}, u32[]{:S(2)}) collective-permute-start(f32[384,1024]{1,0:T(8,128)S(1)} %copy-done.7), channel_id=1, source_target_pairs={{8,16},{20,12},{9,17},{21,13},{10,18},{22,14},{11,19},{23,15}} | collective-permute-start | bytes 4718600 | tf_op jit(solution)/shard_map/ppermute | solution.py:100
  108.5 9.9 %copy-start.6 = (f32[768,768]{1,0:T(8,128)S(1)}, f32[768,768]{1,0:T(8,128)}, u32[]{:S(2)}) copy-start(f32[768,768]{1,0:T(8,128)} %copy-done.5) | copy-start | bytes 7077892
  108.5 79.9 %slice-start = ((s8[7077888]{0:T(1024)(128)(4,1)}), s8[4194304]{0:T(1024)(128)(4,1)S(1)}, s32[]{:S(2)}) async-start(s8[7077888]{0:T(1024)(128)(4,1)} %bitcast.55), calls=%async_computation | async-start | bytes 8388608
  110.0 31.4 %collective-permute-start.4 = (f32[288,1024]{1,0:T(8,128)}, f32[288,1024]{1,0:T(8,128)}, u32[]{:S(2)}, u32[]{:S(2)}) collective-permute-start(f32[288,1024]{1,0:T(8,128)} %slice.87), channel_id=1, source_target_pairs={{0,24},{4,12},{8,0},{12,20},{16,8},{20,28},{24,16},{28,4},{1,25},{... | collective-permute-start | bytes 3538952 | tf_op jit(solution)/shard_map/ppermute | solution.py:100
  112.5 82.1 %collective-permute-start.7 = (f32[384,1024]{1,0:T(8,128)S(1)}, f32[384,1024]{1,0:T(8,128)}, u32[]{:S(2)}, u32[]{:S(2)}) collective-permute-start(f32[384,1024]{1,0:T(8,128)S(1)} %copy-done.7), channel_id=1, source_target_pairs={{0,8},{4,28},{12,4},{16,24},{24,0},{28,20},{1,9},{5,29},{13,5},{17... | collective-permute-start | bytes 4718600 | tf_op jit(solution)/shard_map/ppermute | solution.py:100
  118.4 5.8 %copy-start.4 = (f32[768,1024]{1,0:T(8,128)S(1)}, f32[768,1024]{1,0:T(8,128)}, u32[]{:S(2)}) copy-start(f32[768,1024]{1,0:T(8,128)} %fusion.14) | copy-start | bytes 9437188
  118.4 70.1 %slice-start.1 = ((s8[7077888]{0:T(1024)(128)(4,1)}), s8[2883584]{0:T(1024)(128)(4,1)S(1)}, s32[]{:S(2)}) async-start(s8[7077888]{0:T(1024)(128)(4,1)} %bitcast.55), calls=%async_computation.1 | async-start | bytes 5767168
  141.4 57.5 %collective-permute-start.12 = (f32[192,1024]{1,0:T(8,128)S(1)}, f32[192,1024]{1,0:T(8,128)}, u32[]{:S(2)}, u32[]{:S(2)}) collective-permute-start(f32[192,1024]{1,0:T(8,128)S(1)} %bitcast.57), channel_id=1, source_target_pairs={{0,16},{4,20},{24,8},{28,12},{1,17},{5,21},{25,9},{29,13},{2,18},{... | collective-permute-start | bytes 2359304 | tf_op jit(solution)/shard_map/ppermute | solution.py:18
  185.1 30.5 %collective-permute-start.13 = (f32[192,1024]{1,0:T(8,128)S(1)}, f32[192,1024]{1,0:T(8,128)}, u32[]{:S(2)}, u32[]{:S(2)}) collective-permute-start(f32[192,1024]{1,0:T(8,128)S(1)} %bitcast.58), channel_id=1, source_target_pairs={{8,24},{12,28},{16,0},{20,4},{9,25},{13,29},{17,1},{21,5},{10,26},... | collective-permute-start | bytes 2359304 | tf_op jit(solution)/shard_map/ppermute | solution.py:18
  186.4 39.7 %collective-permute-start.8 = (f32[384,1024]{1,0:T(8,128)}, f32[384,1024]{1,0:T(8,128)}, u32[]{:S(2)}, u32[]{:S(2)}) collective-permute-start(f32[384,1024]{1,0:T(8,128)} %collective-permute-done.3), channel_id=1, source_target_pairs={{0,4},{4,0},{8,12},{12,8},{16,20},{20,16},{24,28},{28,24},{1,5},{5... | collective-permute-start | bytes 4718600 | tf_op jit(solution)/shard_map/ppermute | solution.py:18
  194.6 31.4 %collective-permute-start.9 = (f32[288,1024]{1,0:T(8,128)}, f32[288,1024]{1,0:T(8,128)S(1)}, u32[]{:S(2)}, u32[]{:S(2)}) collective-permute-start(f32[288,1024]{1,0:T(8,128)} %collective-permute-done.4), channel_id=1, source_target_pairs={{0,4},{4,0},{8,12},{12,8},{16,20},{20,16},{24,28},{28,24},{1,5},{5... | collective-permute-start | bytes 3538952 | tf_op jit(solution)/shard_map/ppermute | solution.py:18
  198.9 35.6 %collective-permute-start.14 = (f32[96,1024]{1,0:T(8,128)}, f32[96,1024]{1,0:T(8,128)S(1)}, u32[]{:S(2)}, u32[]{:S(2)}) collective-permute-start(f32[96,1024]{1,0:T(8,128)} %slice.88), channel_id=1, source_target_pairs={{0,8},{4,28},{8,16},{12,4},{16,24},{20,12},{24,0},{28,20},{1,9},{5... | collective-permute-start | bytes 1179656 | tf_op jit(solution)/shard_map/ppermute | solution.py:100
  233.5 3.3 %copy-start.1 = (f32[1,768,192]{1,2,0:T(8,128)S(1)}, f32[1,768,192]{1,2,0:T(8,128)}, u32[]{:S(2)}) copy-start(f32[1,768,192]{1,2,0:T(8,128)} %param.11) | copy-start | bytes 1769476

commit v4 on v3

--- a/solution.py
+++ b/solution.py
@@ -73,6 +73,27 @@
     )(*operands)
 
 
+def copy_rows(from_ref, to_ref, sem):
+    copy = pltpu.make_async_copy(from_ref.at[pl.ds(0, to_ref.shape[0])], to_ref, sem)
+    copy.start()
+    copy.wait()
+
+
+def first_rows(value, rows):
+    shape = (rows, value.shape[1])
+    return pl.pallas_call(
+        copy_rows,
+        out_shape=pltpu.VMEM(shape, value.dtype),
+        in_specs=[pl.BlockSpec(memory_space=pl.ANY)],
+        out_specs=pl.BlockSpec(memory_space=pltpu.VMEM),
+        scratch_shapes=[pltpu.SemaphoreType.DMA(())],
+        cost_estimate=pl.CostEstimate(
+            flops=0, bytes_accessed=8 * rows * shape[1], transcendentals=0
+        ),
+        compiler_params=pltpu.CompilerParams(vmem_limit_bytes=8 << 20),
+    )(value)
+
+
 def per_device(charges, near_blocks, neighbours, compress, transfer, expand):
     count = lax.axis_size("leaf")
     here = lax.axis_index("leaf")
@@ -106,7 +127,8 @@
     coeffs = jnp.einsum("ar,ac->rc", compress[0], charges, precision=HIGH)
     later, coeffs = lax.optimization_barrier((charges, coeffs))
     for part, (low, high) in enumerate(cuts):
-        far.append(move((later if part else charges)[low:high], two_along(1, count)))
+        rows = later[low:high] if part else first_rows(charges, high)
+        far.append(move(rows, two_along(1, count)))
         relay.append(partner(far[part], 0))
     low, high = cuts[0]
     near_central = move(later[low:high], central)

time: 239 us -> 239 us (level)
  matrix products: 51.1 us -> 47.9 us
  waiting for transfers between devices: 88.6 us -> 91.2 us
    ppermute x8, waiting for transfers between devices: 72.9 us -> 75.3 us  [partner(): lax.ppermute(value, 'leaf', [(i, i ^ 1 << distance) for i in senders or e...]
  transfers between devices with their start and end apart: 15 -> 15, of which waited for: 4 -> 4; matrix products, arithmetic and copies ran while one was open for 29% -> 27% of each run, Pallas kernels for 0% -> 0%
where the time goes in v4:
time: 239 us; the launch traced here: 236 us
  waiting for transfers between devices  91.2 us (38%)
  starting transfers between devices  72.3 us (30%)
  matrix products  47.9 us (20%)
  other arithmetic  11.4 us (5%)
  between operations  5.61 us (2%)
  local copies, waits for them, and re-layouts  5.37 us (2%)
  Pallas kernels  2.45 us (1%)
    ppermute x8, waiting for transfers between devices, partner(): lax.ppermute(value, 'leaf', [(i, i ^ 1 << distance) for i in senders or e...  75.3 us
    ppermute x8, starting transfers between devices, partner(): lax.ppermute(value, 'leaf', [(i, i ^ 1 << distance) for i in senders or e...  52.8 us
    dot_general x14, matrix products, dot(): return jnp.dot(a, b, precision=HIGH)  44.5 us
    ppermute x7, starting transfers between devices, move(): return lax.ppermute(value, 'leaf', pairs)  19.5 us
    ppermute x7, waiting for transfers between devices, move(): return lax.ppermute(value, 'leaf', pairs)  15.9 us
    add x5, other arithmetic, add(): return lax.optimization_barrier(total + dot(a, b))  4.79 us
  transfers between devices with their start and end apart: 15, of which 4 were waited for; matrix products, arithmetic and copies ran while one was open for 27% of the time, Pallas kernels for 0%

profile of v4, /device:TPU:0, one launch (start us, length us, event | category | flops | bytes accessed | tf_op | source)
XLA Modules:
  0.0 236.3 jit_solution(13877979517374966266)
XLA Ops:
  0.0 3.0 %collective-permute-start.2 = (f32[768,1024]{1,0:T(8,128)}, f32[768,1024]{1,0:T(8,128)}, u32[]{:S(2)}, u32[]{:S(2)}) collective-permute-start(f32[768,1024]{1,0:T(8,128)} %from_ref.1), channel_id=1, source_target_pairs={{0,4},{4,0},{8,12},{12,8},{16,20},{20,16},{24,28},{28,24},{1,5},{5... | collective-permute-start | bytes 9437192 | tf_op jit(solution)/shard_map/ppermute | solution.py:18
  3.0 3.3 %fusion.49 = f32[192,1024]{1,0:T(8,128)S(1)} fusion(f32[768,1024]{1,0:T(8,128)} %from_ref.1, f32[1,768,192]{1,2,0:T(8,128)} %param.9), kind=kOutput, calls=%fused_computation.50 | convolution fusion | flops 905969664 | bytes 4521984 | tf_op jit(solution)/shard_map/ar,ac->rc/dot_general | solution.py:127
  7.3 4.3 %collective-permute-start.5 = (f32[96,1024]{1,0:T(8,128)}, f32[96,1024]{1,0:T(8,128)}, u32[]{:S(2)}, u32[]{:S(2)}) collective-permute-start(f32[96,1024]{1,0:T(8,128)} %slice.84), channel_id=1, source_target_pairs={{0,24},{4,12},{8,0},{12,20},{16,8},{20,28},{24,16},{28,4},{1,25},{... | collective-permute-start | bytes 1179656 | tf_op jit(solution)/shard_map/ppermute | solution.py:121
  13.4 1.6 collective-permute-start.11
  18.1 4.3 %select_bitcast_fusion = (f32[768,768]{1,0:T(8,128)}, f32[768,768]{1,0:T(8,128)S(1)}) fusion(f32[1,3,768,768]{3,2,1,0:T(8,128)} %param.7, pred[]{:T(512)S(6)} %eq.47, pred[]{:T(512)S(6)} %eq.46, pred[]{:T(512)S(6)} %eq.43, pred[]{:T(512)S(6)} %eq.42), kind=kLoop, calls=%fused_computation.16 | loop fusion | flops 2359296 | bytes 9437188 | tf_op jit(solution)/shard_map/jit(_where)/select_n | solution.py:118
  23.9 7.2 %fusion.14 = f32[768,1024]{1,0:T(8,128)} fusion(f32[768,1024]{1,0:T(8,128)S(1)} %copy-done.3, f32[1,3,768,768]{3,2,1,0:T(8,128)} %param.7), kind=kOutput, calls=%fused_computation.14 | convolution fusion | flops 3623878656 | bytes 8650752 | tf_op jit(solution)/shard_map/dot_general | solution.py:13
  31.1 57.1 %collective-permute-done = f32[192,1024]{1,0:T(8,128)} collective-permute-done((f32[192,1024]{1,0:T(8,128)S(1)}, f32[192,1024]{1,0:T(8,128)}, u32[]{:S(2)}, u32[]{:S(2)}) %collective-permute-start) | collective-permute-done | bytes 786464 | tf_op jit(solution)/shard_map/ppermute | solution.py:18
  88.3 1.6 convolution_add_fusion.2
  89.9 1.9 collective-permute-start.1
  94.3 2.7 %slice.86 = f32[384,1024]{1,0:T(8,128)} slice(f32[768,1024]{1,0:T(8,128)} %from_ref.1), slice={[0:384], [0:1024]} | slice | bytes 3145728 | tf_op jit(solution)/shard_map/slice | solution.py:134
  97.1 1.5 collective-permute-start.10
  98.6 1.3 pad_maximum_fusion.left_ref
  100.7 6.3 %collective-permute-done.10 = f32[96,1024]{1,0:T(8,128)S(1)} collective-permute-done((f32[96,1024]{1,0:T(8,128)}, f32[96,1024]{1,0:T(8,128)S(1)}, u32[]{:S(2)}, u32[]{:S(2)}) %collective-permute-start.10) | collective-permute-done | bytes 393248 | tf_op jit(solution)/shard_map/ppermute | solution.py:18
  107.8 1.5 fusion.53
  109.3 2.5 %collective-permute-start.4 = (f32[288,1024]{1,0:T(8,128)}, f32[288,1024]{1,0:T(8,128)}, u32[]{:S(2)}, u32[]{:S(2)}) collective-permute-start(f32[288,1024]{1,0:T(8,128)} %slice.83), channel_id=1, source_target_pairs={{0,24},{4,12},{8,0},{12,20},{16,8},{20,28},{24,16},{28,4},{1,25},{... | collective-permute-start | bytes 3538952 | tf_op jit(solution)/shard_map/ppermute | solution.py:121
  111.8 4.2 %collective-permute-start.7 = (f32[384,1024]{1,0:T(8,128)S(1)}, f32[384,1024]{1,0:T(8,128)}, u32[]{:S(2)}, u32[]{:S(2)}) collective-permute-start(f32[384,1024]{1,0:T(8,128)S(1)} %copy-done.8), channel_id=1, source_target_pairs={{0,8},{4,28},{12,4},{16,24},{24,0},{28,20},{1,9},{5,29},{13,5},{17... | collective-permute-start | bytes 4718600 | tf_op jit(solution)/shard_map/ppermute | solution.py:121
  116.0 1.4 fusion.60
  117.4 4.1 %fusion.35 = f32[768,1024]{1,0:T(8,128)S(1)} fusion(f32[288,1024]{1,0:T(8,128)} %collective-permute-done.11, f32[768,768]{1,0:T(8,128)S(1)} %copy-done.7), kind=kOutput, calls=%fused_computation.35 | convolution fusion | flops 1358954496 | bytes 5505024 | tf_op jit(solution)/shard_map/dot_general | solution.py:13
  121.6 1.6 convolution_add_fusion.1
  123.2 1.5 convolution_add_fusion
  124.8 15.9 %collective-permute-done.4 = f32[288,1024]{1,0:T(8,128)} collective-permute-done((f32[288,1024]{1,0:T(8,128)}, f32[288,1024]{1,0:T(8,128)}, u32[]{:S(2)}, u32[]{:S(2)}) %collective-permute-start.4) | collective-permute-done | bytes 1179680 | tf_op jit(solution)/shard_map/ppermute | solution.py:121
  140.7 42.9 %collective-permute-start.12 = (f32[192,1024]{1,0:T(8,128)S(1)}, f32[192,1024]{1,0:T(8,128)S(1)}, u32[]{:S(2)}, u32[]{:S(2)}) collective-permute-start(f32[192,1024]{1,0:T(8,128)S(1)} %bitcast.58), channel_id=1, source_target_pairs={{0,16},{4,20},{24,8},{28,12},{1,17},{5,21},{25,9},{29,13},{2,18},{... | collective-permute-start | bytes 2359304 | tf_op jit(solution)/shard_map/ppermute | solution.py:18
  183.5 1.3 collective-permute-start.13
  184.9 2.0 collective-permute-start.8
  186.9 6.2 %fusion = f32[768,1024]{1,0:T(8,128)S(1)} fusion(f32[96,1024]{1,0:T(8,128)} %collective-permute-done.5, f32[288,1024]{1,0:T(8,128)} %collective-permute-done.4, f32[384,1024]{1,0:T(8,128)} %collective-permute-done.3, f32[1,3,768,768]{3,2,1,0:T(8,128)S(1)} %bitcast.56, pred[]{:T(512)S(6)} %eq.41, pred[]{:T(512)S(6)} %eq.40), kind=kOutput, calls=%fused_computation | convolution fusion | flops 3626631168 | bytes 11010050 | tf_op jit(solution)/shard_map/dot_general | solution.py:13
  193.2 4.1 %fusion.33 = f32[768,1024]{1,0:T(8,128)S(1)} fusion(f32[384,1024]{1,0:T(8,128)S(1)} %collective-permute-done.6, f32[384,1024]{1,0:T(8,128)} %collective-permute-done.7, f32[768,768]{1,0:T(8,128)S(1)} %copy-done.7, pred[]{:T(512)S(6)} %or.3), kind=kOutput, calls=%fused_computation.30 | convolution fusion | flops 1812332544 | bytes 7471105 | tf_op jit(solution)/shard_map/dot_general | solution.py:13
  197.3 5.7 %collective-permute-start.14 = (f32[96,1024]{1,0:T(8,128)}, f32[96,1024]{1,0:T(8,128)S(1)}, u32[]{:S(2)}, u32[]{:S(2)}) collective-permute-start(f32[96,1024]{1,0:T(8,128)} %slice.84), channel_id=1, source_target_pairs={{0,8},{4,28},{8,16},{12,4},{16,24},{20,12},{24,0},{28,20},{1,9},{5... | collective-permute-start | bytes 1179656 | tf_op jit(solution)/shard_map/ppermute | solution.py:121
  203.0 11.8 %collective-permute-done.13 = f32[192,1024]{1,0:T(8,128)} collective-permute-done((f32[192,1024]{1,0:T(8,128)S(1)}, f32[192,1024]{1,0:T(8,128)}, u32[]{:S(2)}, u32[]{:S(2)}) %collective-permute-start.13) | collective-permute-done | bytes 786464 | tf_op jit(solution)/shard_map/ppermute | solution.py:18
  214.9 2.6 %fusion.44 = f32[768,1024]{1,0:T(8,128)S(1)} fusion(f32[192,1024]{1,0:T(8,128)S(1)} %collective-permute-done.12, f32[192,1024]{1,0:T(8,128)} %collective-permute-done.13, f32[768,384]{0,1:T(8,128)S(1)} %convolution_bitcast_fusion, pred[]{:T(512)S(6)} %and.16), kind=kOutput, calls=%fused_computation.44 | convolution fusion | flops 906166272 | bytes 5308417 | tf_op jit(solution)/shard_map/dot_general | solution.py:13
  217.5 5.9 %fusion.30 = f32[768,1024]{1,0:T(8,128)S(1)} fusion(f32[768,1024]{1,0:T(8,128)S(1)} %convolution_add_fusion, f32[768,1024]{1,0:T(8,128)} %collective-permute-done.2, f32[1,3,768,768]{3,2,1,0:T(8,128)S(1)} %bitcast.56, pred[]{:T(512)S(6)} %eq.39, pred[]{:T(512)S(6)} %eq.38), kind=kOutput, calls=%fused_computation.29 | convolution fusion | flops 3625844736 | bytes 14155778 | tf_op jit(solution)/shard_map/dot_general | solution.py:13
  225.4 5.4 %fusion.25 = f32[768,1024]{1,0:T(8,128)S(1)} fusion(f32[768,1024]{1,0:T(8,128)S(1)} %add.55, f32[288,1024]{1,0:T(8,128)S(1)} %collective-permute-done.9, f32[384,1024]{1,0:T(8,128)} %collective-permute-done.8, f32[768,768]{1,0:T(8,128)S(1)} %copy-done.5), kind=kOutput, calls=%fused_computation.28 | convolution fusion | flops 3172368384 | bytes 11403264 | tf_op jit(solution)/shard_map/dot_general | solution.py:13
  233.7 2.3 shard_map.65
  (56 shorter events, 11.4 us)
Async XLA Ops:
  0.0 99.9 %copy-start = (f32[1,768,192]{1,2,0:T(8,128)S(1)}, f32[1,768,192]{1,2,0:T(8,128)}, u32[]{:S(2)}) copy-start(f32[1,768,192]{1,2,0:T(8,128)} %param.11) | copy-start | bytes 1769476
  0.0 6.5 %copy-start.2 = (f32[768,1024]{1,0:T(8,128)S(1)}, f32[768,1024]{1,0:T(8,128)}, u32[]{:S(2)}) copy-start(f32[768,1024]{1,0:T(8,128)} %from_ref.1) | copy-start | bytes 9437188
  0.0 217.5 %collective-permute-start.2 = (f32[768,1024]{1,0:T(8,128)}, f32[768,1024]{1,0:T(8,128)}, u32[]{:S(2)}, u32[]{:S(2)}) collective-permute-start(f32[768,1024]{1,0:T(8,128)} %from_ref.1), channel_id=1, source_target_pairs={{0,4},{4,0},{8,12},{12,8},{16,20},{20,16},{24,28},{28,24},{1,5},{5... | collective-permute-start | bytes 9437192 | tf_op jit(solution)/shard_map/ppermute | solution.py:18
  6.3 81.9 %collective-permute-start = (f32[192,1024]{1,0:T(8,128)S(1)}, f32[192,1024]{1,0:T(8,128)}, u32[]{:S(2)}, u32[]{:S(2)}) collective-permute-start(f32[192,1024]{1,0:T(8,128)S(1)} %fusion.49), channel_id=1, source_target_pairs={{0,4},{4,0},{8,12},{12,8},{16,20},{20,16},{24,28},{28,24},{1,5},{5... | collective-permute-start | bytes 2359304 | tf_op jit(solution)/shard_map/ppermute | solution.py:18
  7.3 89.7 %collective-permute-start.5 = (f32[96,1024]{1,0:T(8,128)}, f32[96,1024]{1,0:T(8,128)}, u32[]{:S(2)}, u32[]{:S(2)}) collective-permute-start(f32[96,1024]{1,0:T(8,128)} %slice.84), channel_id=1, source_target_pairs={{0,24},{4,12},{8,0},{12,20},{16,8},{20,28},{24,16},{28,4},{1,25},{... | collective-permute-start | bytes 1179656 | tf_op jit(solution)/shard_map/ppermute | solution.py:121
  11.7 3.2 %copy-start.10 = (s32[1,2]{1,0:T(1,128)S(1)}, s32[1,2]{1,0:T(1,128)}, u32[]{:S(2)}) copy-start(s32[1,2]{1,0:T(1,128)} %param.8) | copy-start | bytes 28
  11.8 171.8 %collective-permute-start.3 = (f32[384,1024]{1,0:T(8,128)S(1)}, f32[384,1024]{1,0:T(8,128)}, u32[]{:S(2)}, u32[]{:S(2)}) collective-permute-start(f32[384,1024]{1,0:T(8,128)S(1)} %shard_map.64), channel_id=1, source_target_pairs={{0,24},{4,12},{8,0},{12,20},{16,8},{20,28},{24,16},{28,4},{1,25},{... | collective-permute-start | bytes 4718600 | tf_op jit(solution)/shard_map/ppermute | solution.py:121
  13.4 95.9 %collective-permute-start.11 = (f32[288,1024]{1,0:T(8,128)}, f32[288,1024]{1,0:T(8,128)}, u32[]{:S(2)}, u32[]{:S(2)}) collective-permute-start(f32[288,1024]{1,0:T(8,128)} %slice.83), channel_id=1, source_target_pairs={{0,8},{4,28},{8,16},{12,4},{16,24},{20,12},{24,0},{28,20},{1,9},{5... | collective-permute-start | bytes 3538952 | tf_op jit(solution)/shard_map/ppermute | solution.py:121
  18.1 5.3 %copy-start.9 = (f32[1,3,2,192,192]{4,3,2,1,0:T(8,128)S(1)}, f32[1,3,2,192,192]{4,3,2,1,0:T(8,128)}, u32[]{:S(2)}) copy-start(f32[1,3,2,192,192]{4,3,2,1,0:T(8,128)} %param.10) | copy-start | bytes 2654212
  18.1 5.8 %copy-start.3 = (f32[768,1024]{1,0:T(8,128)S(1)}, f32[768,1024]{1,0:T(8,128)}, u32[]{:S(2)}) copy-start(f32[768,1024]{1,0:T(8,128)} %from_ref.1) | copy-start | bytes 9437188
  22.4 8.7 %copy-start.6 = (f32[768,768]{1,0:T(8,128)}, f32[768,768]{1,0:T(8,128)S(1)}, u32[]{:S(2)}) copy-start(f32[768,768]{1,0:T(8,128)S(1)} %get-tuple-element.10) | copy-start | bytes 7077892
  89.9 21.9 %collective-permute-start.1 = (f32[192,1024]{1,0:T(8,128)S(1)}, f32[192,1024]{1,0:T(8,128)}, u32[]{:S(2)}, u32[]{:S(2)}) collective-permute-start(f32[192,1024]{1,0:T(8,128)S(1)} %bitcast.57), channel_id=1, source_target_pairs={{0,8},{4,12},{8,0},{12,4},{16,24},{20,28},{24,16},{28,20},{1,9},{5... | collective-permute-start | bytes 2359304 | tf_op jit(solution)/shard_map/ppermute | solution.py:18
  97.1 10.7 %copy-start.5 = (f32[768,768]{1,0:T(8,128)S(1)}, f32[768,768]{1,0:T(8,128)}, u32[]{:S(2)}) copy-start(f32[768,768]{1,0:T(8,128)} %get-tuple-element.9) | copy-start | bytes 7077892
  97.1 9.9 %collective-permute-start.10 = (f32[96,1024]{1,0:T(8,128)}, f32[96,1024]{1,0:T(8,128)S(1)}, u32[]{:S(2)}, u32[]{:S(2)}) collective-permute-start(f32[96,1024]{1,0:T(8,128)} %collective-permute-done.5), channel_id=1, source_target_pairs={{0,4},{4,0},{8,12},{12,8},{16,20},{20,16},{24,28},{28,24},{1,5},{5... | collective-permute-start | bytes 1179656 | tf_op jit(solution)/shard_map/ppermute | solution.py:18
  100.7 11.1 %copy-start.8 = (f32[384,1024]{1,0:T(8,128)S(1)}, f32[384,1024]{1,0:T(8,128)}, u32[]{:S(2)}) copy-start(f32[384,1024]{1,0:T(8,128)} %slice.86) | copy-start | bytes 4718596
  107.0 77.9 %collective-permute-start.6 = (f32[384,1024]{1,0:T(8,128)}, f32[384,1024]{1,0:T(8,128)S(1)}, u32[]{:S(2)}, u32[]{:S(2)}) collective-permute-start(f32[384,1024]{1,0:T(8,128)} %slice.86), channel_id=1, source_target_pairs={{8,16},{20,12},{9,17},{21,13},{10,18},{22,14},{11,19},{23,15}} | collective-permute-start | bytes 4718600 | tf_op jit(solution)/shard_map/ppermute | solution.py:121
  107.7 9.7 %copy-start.7 = (f32[768,768]{1,0:T(8,128)S(1)}, f32[768,768]{1,0:T(8,128)}, u32[]{:S(2)}) copy-start(f32[768,768]{1,0:T(8,128)} %copy-done.6) | copy-start | bytes 7077892
  107.8 79.1 %slice-start = ((s8[7077888]{0:T(1024)(128)(4,1)}), s8[4194304]{0:T(1024)(128)(4,1)S(1)}, s32[]{:S(2)}) async-start(s8[7077888]{0:T(1024)(128)(4,1)} %bitcast.55), calls=%async_computation | async-start | bytes 8388608
  109.3 31.4 %collective-permute-start.4 = (f32[288,1024]{1,0:T(8,128)}, f32[288,1024]{1,0:T(8,128)}, u32[]{:S(2)}, u32[]{:S(2)}) collective-permute-start(f32[288,1024]{1,0:T(8,128)} %slice.83), channel_id=1, source_target_pairs={{0,24},{4,12},{8,0},{12,20},{16,8},{20,28},{24,16},{28,4},{1,25},{... | collective-permute-start | bytes 3538952 | tf_op jit(solution)/shard_map/ppermute | solution.py:121
  111.8 81.2 %collective-permute-start.7 = (f32[384,1024]{1,0:T(8,128)S(1)}, f32[384,1024]{1,0:T(8,128)}, u32[]{:S(2)}, u32[]{:S(2)}) collective-permute-start(f32[384,1024]{1,0:T(8,128)S(1)} %copy-done.8), channel_id=1, source_target_pairs={{0,8},{4,28},{12,4},{16,24},{24,0},{28,20},{1,9},{5,29},{13,5},{17... | collective-permute-start | bytes 4718600 | tf_op jit(solution)/shard_map/ppermute | solution.py:121
  117.4 5.8 %copy-start.4 = (f32[768,1024]{1,0:T(8,128)S(1)}, f32[768,1024]{1,0:T(8,128)}, u32[]{:S(2)}) copy-start(f32[768,1024]{1,0:T(8,128)} %fusion.14) | copy-start | bytes 9437188
  117.4 69.4 %slice-start.1 = ((s8[7077888]{0:T(1024)(128)(4,1)}), s8[2883584]{0:T(1024)(128)(4,1)S(1)}, s32[]{:S(2)}) async-start(s8[7077888]{0:T(1024)(128)(4,1)} %bitcast.55), calls=%async_computation.1 | async-start | bytes 5767168
  140.7 56.7 %collective-permute-start.12 = (f32[192,1024]{1,0:T(8,128)S(1)}, f32[192,1024]{1,0:T(8,128)S(1)}, u32[]{:S(2)}, u32[]{:S(2)}) collective-permute-start(f32[192,1024]{1,0:T(8,128)S(1)} %bitcast.58), channel_id=1, source_target_pairs={{0,16},{4,20},{24,8},{28,12},{1,17},{5,21},{25,9},{29,13},{2,18},{... | collective-permute-start | bytes 2359304 | tf_op jit(solution)/shard_map/ppermute | solution.py:18
  183.5 31.3 %collective-permute-start.13 = (f32[192,1024]{1,0:T(8,128)S(1)}, f32[192,1024]{1,0:T(8,128)}, u32[]{:S(2)}, u32[]{:S(2)}) collective-permute-start(f32[192,1024]{1,0:T(8,128)S(1)} %bitcast.59), channel_id=1, source_target_pairs={{8,24},{12,28},{16,0},{20,4},{9,25},{13,29},{17,1},{21,5},{10,26},... | collective-permute-start | bytes 2359304 | tf_op jit(solution)/shard_map/ppermute | solution.py:18
  184.9 40.5 %collective-permute-start.8 = (f32[384,1024]{1,0:T(8,128)}, f32[384,1024]{1,0:T(8,128)}, u32[]{:S(2)}, u32[]{:S(2)}) collective-permute-start(f32[384,1024]{1,0:T(8,128)} %collective-permute-done.3), channel_id=1, source_target_pairs={{0,4},{4,0},{8,12},{12,8},{16,20},{20,16},{24,28},{28,24},{1,5},{5... | collective-permute-start | bytes 4718600 | tf_op jit(solution)/shard_map/ppermute | solution.py:18
  193.1 32.3 %collective-permute-start.9 = (f32[288,1024]{1,0:T(8,128)}, f32[288,1024]{1,0:T(8,128)S(1)}, u32[]{:S(2)}, u32[]{:S(2)}) collective-permute-start(f32[288,1024]{1,0:T(8,128)} %collective-permute-done.4), channel_id=1, source_target_pairs={{0,4},{4,0},{8,12},{12,8},{16,20},{20,16},{24,28},{28,24},{1,5},{5... | collective-permute-start | bytes 3538952 | tf_op jit(solution)/shard_map/ppermute | solution.py:18
  197.3 36.4 %collective-permute-start.14 = (f32[96,1024]{1,0:T(8,128)}, f32[96,1024]{1,0:T(8,128)S(1)}, u32[]{:S(2)}, u32[]{:S(2)}) collective-permute-start(f32[96,1024]{1,0:T(8,128)} %slice.84), channel_id=1, source_target_pairs={{0,8},{4,28},{8,16},{12,4},{16,24},{20,12},{24,0},{28,20},{1,9},{5... | collective-permute-start | bytes 1179656 | tf_op jit(solution)/shard_map/ppermute | solution.py:121
  232.7 3.3 %copy-start.1 = (f32[1,768,192]{1,2,0:T(8,128)S(1)}, f32[1,768,192]{1,2,0:T(8,128)}, u32[]{:S(2)}) copy-start(f32[1,768,192]{1,2,0:T(8,128)} %param.11) | copy-start | bytes 1769476

commit v5 on v4

--- a/solution.py
+++ b/solution.py
@@ -124,15 +124,15 @@
         return lax.optimization_barrier(total + dot(a, b))
 
     far, near, relay = [], [], []
+    leading_rows = first_rows(charges, cuts[0][1])
     coeffs = jnp.einsum("ar,ac->rc", compress[0], charges, precision=HIGH)
     later, coeffs = lax.optimization_barrier((charges, coeffs))
     for part, (low, high) in enumerate(cuts):
-        rows = later[low:high] if part else first_rows(charges, high)
+        rows = later[low:high] if part else leading_rows
         far.append(move(rows, two_along(1, count)))
         relay.append(partner(far[part], 0))
-    low, high = cuts[0]
-    near_central = move(later[low:high], central)
-    near_others = move(later[low:high], others)
+    near_central = move(leading_rows, central)
+    near_others = move(leading_rows, others)
     near.append(jnp.where(over_middle, near_central, near_others))
     for part, (low, high) in enumerate(cuts[1:], 1):
         near.append(move(later[low:high], shift))

time: 239 us -> 236 us (0.987)
  local copies, waits for them, and re-layouts: 5.37 us -> 2.61 us
    slice x3 -> x2, local copies, waits for them, and re-layouts: 4.64 us -> 1.92 us  [per_device(): rows = later[low:high] if part else leading_rows]
  transfers between devices with their start and end apart: 15 -> 15, of which waited for: 4 -> 4; matrix products, arithmetic and copies ran while one was open for 27% -> 26% of each run, Pallas kernels for 0% -> 0%
where the time goes in v5:
time: 236 us; the launch traced here: 233 us
  waiting for transfers between devices  91.5 us (39%)
  starting transfers between devices  72.2 us (31%)
  matrix products  46.8 us (20%)
  other arithmetic  11.4 us (5%)
  between operations  5.55 us (2%)
  local copies, waits for them, and re-layouts  2.61 us (1%)
  Pallas kernels  2.44 us (1%)
    ppermute x8, waiting for transfers between devices, partner(): lax.ppermute(value, 'leaf', [(i, i ^ 1 << distance) for i in senders or e...  77 us
    ppermute x8, starting transfers between devices, partner(): lax.ppermute(value, 'leaf', [(i, i ^ 1 << distance) for i in senders or e...  53.4 us
    dot_general x14, matrix products, dot(): return jnp.dot(a, b, precision=HIGH)  43.4 us
    ppermute x7, starting transfers between devices, move(): return lax.ppermute(value, 'leaf', pairs)  18.9 us
    ppermute x7, waiting for transfers between devices, move(): return lax.ppermute(value, 'leaf', pairs)  14.5 us
    add x5, other arithmetic, add(): return lax.optimization_barrier(total + dot(a, b))  4.79 us
  transfers between devices with their start and end apart: 15, of which 4 were waited for; matrix products, arithmetic and copies ran while one was open for 26% of the time, Pallas kernels for 0%

profile of v5, /device:TPU:0, one launch (start us, length us, event | category | flops | bytes accessed | tf_op | source)
XLA Modules:
  0.0 232.5 jit_solution(6188237927892227507)
XLA Ops:
  0.0 3.0 %collective-permute-start.2 = (f32[768,1024]{1,0:T(8,128)}, f32[768,1024]{1,0:T(8,128)}, u32[]{:S(2)}, u32[]{:S(2)}) collective-permute-start(f32[768,1024]{1,0:T(8,128)} %from_ref.1), channel_id=1, source_target_pairs={{0,4},{4,0},{8,12},{12,8},{16,20},{20,16},{24,28},{28,24},{1,5},{5... | collective-permute-start | bytes 9437192 | tf_op jit(solution)/shard_map/ppermute | solution.py:18
  3.0 3.3 %fusion.49 = f32[192,1024]{1,0:T(8,128)S(1)} fusion(f32[768,1024]{1,0:T(8,128)} %from_ref.1, f32[1,768,192]{1,2,0:T(8,128)} %param.9), kind=kOutput, calls=%fused_computation.50 | convolution fusion | flops 905969664 | bytes 4521984 | tf_op jit(solution)/shard_map/ar,ac->rc/dot_general | solution.py:128
  7.4 4.3 %collective-permute-start.5 = (f32[96,1024]{1,0:T(8,128)}, f32[96,1024]{1,0:T(8,128)}, u32[]{:S(2)}, u32[]{:S(2)}) collective-permute-start(f32[96,1024]{1,0:T(8,128)} %slice.80), channel_id=1, source_target_pairs={{0,24},{4,12},{8,0},{12,20},{16,8},{20,28},{24,16},{28,4},{1,25},{... | collective-permute-start | bytes 1179656 | tf_op jit(solution)/shard_map/ppermute | solution.py:121
  12.3 1.1 slice.79
  13.4 1.6 collective-permute-start.11
  18.1 4.3 %select_bitcast_fusion = (f32[768,768]{1,0:T(8,128)}, f32[768,768]{1,0:T(8,128)S(1)}) fusion(f32[1,3,768,768]{3,2,1,0:T(8,128)} %param.7, pred[]{:T(512)S(6)} %eq.47, pred[]{:T(512)S(6)} %eq.46, pred[]{:T(512)S(6)} %eq.43, pred[]{:T(512)S(6)} %eq.42), kind=kLoop, calls=%fused_computation.16 | loop fusion | flops 2359296 | bytes 9437188 | tf_op jit(solution)/shard_map/jit(_where)/select_n | solution.py:118
  23.8 7.2 %fusion.14 = f32[768,1024]{1,0:T(8,128)} fusion(f32[768,1024]{1,0:T(8,128)S(1)} %copy-done.3, f32[1,3,768,768]{3,2,1,0:T(8,128)} %param.7), kind=kOutput, calls=%fused_computation.14 | convolution fusion | flops 3623878656 | bytes 8650752 | tf_op jit(solution)/shard_map/dot_general | solution.py:13
  31.1 57.2 %collective-permute-done = f32[192,1024]{1,0:T(8,128)} collective-permute-done((f32[192,1024]{1,0:T(8,128)S(1)}, f32[192,1024]{1,0:T(8,128)}, u32[]{:S(2)}, u32[]{:S(2)}) %collective-permute-start) | collective-permute-done | bytes 786464 | tf_op jit(solution)/shard_map/ppermute | solution.py:18
  88.3 1.6 convolution_add_fusion.2
  89.9 1.9 collective-permute-start.1
  94.3 1.6 collective-permute-start.10
  95.8 1.3 pad_maximum_fusion.left_ref
  98.0 6.3 %collective-permute-done.10 = f32[96,1024]{1,0:T(8,128)S(1)} collective-permute-done((f32[96,1024]{1,0:T(8,128)}, f32[96,1024]{1,0:T(8,128)S(1)}, u32[]{:S(2)}, u32[]{:S(2)}) %collective-permute-start.10) | collective-permute-done | bytes 393248 | tf_op jit(solution)/shard_map/ppermute | solution.py:18
  105.1 1.5 fusion.53
  106.6 2.5 %collective-permute-start.4 = (f32[288,1024]{1,0:T(8,128)}, f32[288,1024]{1,0:T(8,128)}, u32[]{:S(2)}, u32[]{:S(2)}) collective-permute-start(f32[288,1024]{1,0:T(8,128)} %slice.79), channel_id=1, source_target_pairs={{0,24},{4,12},{8,0},{12,20},{16,8},{20,28},{24,16},{28,4},{1,25},{... | collective-permute-start | bytes 3538952 | tf_op jit(solution)/shard_map/ppermute | solution.py:121
  109.1 4.2 %collective-permute-start.7 = (f32[384,1024]{1,0:T(8,128)S(1)}, f32[384,1024]{1,0:T(8,128)S(1)}, u32[]{:S(2)}, u32[]{:S(2)}) collective-permute-start(f32[384,1024]{1,0:T(8,128)S(1)} %shard_map.64), channel_id=1, source_target_pairs={{0,8},{4,28},{12,4},{16,24},{24,0},{28,20},{1,9},{5,29},{13,5},{17... | collective-permute-start | bytes 4718600 | tf_op jit(solution)/shard_map/ppermute | solution.py:121
  113.3 1.4 fusion.60
  114.7 4.1 %fusion.35 = f32[768,1024]{1,0:T(8,128)S(1)} fusion(f32[288,1024]{1,0:T(8,128)} %collective-permute-done.11, f32[768,768]{1,0:T(8,128)S(1)} %copy-done.7), kind=kOutput, calls=%fused_computation.35 | convolution fusion | flops 1358954496 | bytes 5505024 | tf_op jit(solution)/shard_map/dot_general | solution.py:13
  118.9 1.6 convolution_add_fusion.1
  120.5 1.5 convolution_add_fusion
  122.1 14.5 %collective-permute-done.4 = f32[288,1024]{1,0:T(8,128)} collective-permute-done((f32[288,1024]{1,0:T(8,128)}, f32[288,1024]{1,0:T(8,128)}, u32[]{:S(2)}, u32[]{:S(2)}) %collective-permute-start.4) | collective-permute-done | bytes 1179680 | tf_op jit(solution)/shard_map/ppermute | solution.py:121
  136.6 43.4 %collective-permute-start.12 = (f32[192,1024]{1,0:T(8,128)S(1)}, f32[192,1024]{1,0:T(8,128)S(1)}, u32[]{:S(2)}, u32[]{:S(2)}) collective-permute-start(f32[192,1024]{1,0:T(8,128)S(1)} %bitcast.58), channel_id=1, source_target_pairs={{0,16},{4,20},{24,8},{28,12},{1,17},{5,21},{25,9},{29,13},{2,18},{... | collective-permute-start | bytes 2359304 | tf_op jit(solution)/shard_map/ppermute | solution.py:18
  180.0 1.3 collective-permute-start.13
  181.4 7.5 %fusion = f32[768,1024]{1,0:T(8,128)} fusion(f32[96,1024]{1,0:T(8,128)} %collective-permute-done.5, f32[288,1024]{1,0:T(8,128)} %collective-permute-done.4, f32[384,1024]{1,0:T(8,128)} %collective-permute-done.3, f32[1,3,768,768]{3,2,1,0:T(8,128)S(1)} %bitcast.56, pred[]{:T(512)S(6)} %eq.41, pred[]{:T(512)S(6)} %eq.40), kind=kOutput, calls=%fused_computation | convolution fusion | flops 3626631168 | bytes 11010050 | tf_op jit(solution)/shard_map/dot_general | solution.py:13
  188.9 2.0 collective-permute-start.9
  190.9 2.7 %fusion.33 = f32[768,1024]{1,0:T(8,128)S(1)} fusion(f32[384,1024]{1,0:T(8,128)S(1)} %collective-permute-done.6, f32[384,1024]{1,0:T(8,128)S(1)} %collective-permute-done.7, f32[768,768]{1,0:T(8,128)S(1)} %copy-done.7, pred[]{:T(512)S(6)} %or.3), kind=kOutput, calls=%fused_computation.30 | convolution fusion | flops 1812332544 | bytes 7471105 | tf_op jit(solution)/shard_map/dot_general | solution.py:13
  193.6 5.0 %collective-permute-start.14 = (f32[96,1024]{1,0:T(8,128)}, f32[96,1024]{1,0:T(8,128)S(1)}, u32[]{:S(2)}, u32[]{:S(2)}) collective-permute-start(f32[96,1024]{1,0:T(8,128)} %slice.80), channel_id=1, source_target_pairs={{0,8},{4,28},{8,16},{12,4},{16,24},{20,12},{24,0},{28,20},{1,9},{5... | collective-permute-start | bytes 1179656 | tf_op jit(solution)/shard_map/ppermute | solution.py:121
  198.6 13.5 %collective-permute-done.13 = f32[192,1024]{1,0:T(8,128)S(1)} collective-permute-done((f32[192,1024]{1,0:T(8,128)S(1)}, f32[192,1024]{1,0:T(8,128)S(1)}, u32[]{:S(2)}, u32[]{:S(2)}) %collective-permute-start.13) | collective-permute-done | bytes 786464 | tf_op jit(solution)/shard_map/ppermute | solution.py:18
  212.0 1.5 fusion.44
  213.6 6.0 %fusion.30 = f32[768,1024]{1,0:T(8,128)S(1)} fusion(f32[768,1024]{1,0:T(8,128)S(1)} %convolution_add_fusion, f32[768,1024]{1,0:T(8,128)} %collective-permute-done.2, f32[1,3,768,768]{3,2,1,0:T(8,128)S(1)} %bitcast.56, pred[]{:T(512)S(6)} %eq.39, pred[]{:T(512)S(6)} %eq.38), kind=kOutput, calls=%fused_computation.29 | convolution fusion | flops 3625844736 | bytes 14155778 | tf_op jit(solution)/shard_map/dot_general | solution.py:13
  221.6 5.4 %fusion.25 = f32[768,1024]{1,0:T(8,128)S(1)} fusion(f32[768,1024]{1,0:T(8,128)S(1)} %add.55, f32[288,1024]{1,0:T(8,128)S(1)} %collective-permute-done.9, f32[384,1024]{1,0:T(8,128)} %collective-permute-done.8, f32[768,768]{1,0:T(8,128)S(1)} %copy-done.5), kind=kOutput, calls=%fused_computation.28 | convolution fusion | flops 3172368384 | bytes 11403264 | tf_op jit(solution)/shard_map/dot_general | solution.py:13
  230.0 2.3 %shard_map.65 = f32[768,1024]{1,0:T(8,128)} custom-call(f32[768,1024]{1,0:T(8,128)S(1)} %add.60.total_ref, bf16[768,288]{1,0:T(8,128)(2,1)S(1)} %pad_maximum_fusion.left_ref, f32[96,1024]{1,0:T(8,128)S(1)} %collective-permute-done.14.right_ref), custom_call_target="tpu_custom_call" | custom-call | flops 452984832 | bytes 6291456 | tf_op jit(solution)/shard_map/pallas_call | solution.py:60
  (55 shorter events, 10.2 us)
Async XLA Ops:
  0.0 97.2 %copy-start = (f32[1,768,192]{1,2,0:T(8,128)S(1)}, f32[1,768,192]{1,2,0:T(8,128)}, u32[]{:S(2)}) copy-start(f32[1,768,192]{1,2,0:T(8,128)} %param.11) | copy-start | bytes 1769476
  0.0 6.5 %copy-start.2 = (f32[768,1024]{1,0:T(8,128)S(1)}, f32[768,1024]{1,0:T(8,128)}, u32[]{:S(2)}) copy-start(f32[768,1024]{1,0:T(8,128)} %from_ref.1) | copy-start | bytes 9437188
  0.0 213.6 %collective-permute-start.2 = (f32[768,1024]{1,0:T(8,128)}, f32[768,1024]{1,0:T(8,128)}, u32[]{:S(2)}, u32[]{:S(2)}) collective-permute-start(f32[768,1024]{1,0:T(8,128)} %from_ref.1), channel_id=1, source_target_pairs={{0,4},{4,0},{8,12},{12,8},{16,20},{20,16},{24,28},{28,24},{1,5},{5... | collective-permute-start | bytes 9437192 | tf_op jit(solution)/shard_map/ppermute | solution.py:18
  6.3 81.9 %collective-permute-start = (f32[192,1024]{1,0:T(8,128)S(1)}, f32[192,1024]{1,0:T(8,128)}, u32[]{:S(2)}, u32[]{:S(2)}) collective-permute-start(f32[192,1024]{1,0:T(8,128)S(1)} %fusion.49), channel_id=1, source_target_pairs={{0,4},{4,0},{8,12},{12,8},{16,20},{20,16},{24,28},{28,24},{1,5},{5... | collective-permute-start | bytes 2359304 | tf_op jit(solution)/shard_map/ppermute | solution.py:18
  7.4 86.9 %collective-permute-start.5 = (f32[96,1024]{1,0:T(8,128)}, f32[96,1024]{1,0:T(8,128)}, u32[]{:S(2)}, u32[]{:S(2)}) collective-permute-start(f32[96,1024]{1,0:T(8,128)} %slice.80), channel_id=1, source_target_pairs={{0,24},{4,12},{8,0},{12,20},{16,8},{20,28},{24,16},{28,4},{1,25},{... | collective-permute-start | bytes 1179656 | tf_op jit(solution)/shard_map/ppermute | solution.py:121
  11.8 3.2 %copy-start.10 = (s32[1,2]{1,0:T(1,128)S(1)}, s32[1,2]{1,0:T(1,128)}, u32[]{:S(2)}) copy-start(s32[1,2]{1,0:T(1,128)} %param.8) | copy-start | bytes 28
  11.8 168.2 %collective-permute-start.3 = (f32[384,1024]{1,0:T(8,128)S(1)}, f32[384,1024]{1,0:T(8,128)}, u32[]{:S(2)}, u32[]{:S(2)}) collective-permute-start(f32[384,1024]{1,0:T(8,128)S(1)} %shard_map.64), channel_id=1, source_target_pairs={{0,24},{4,12},{8,0},{12,20},{16,8},{20,28},{24,16},{28,4},{1,25},{... | collective-permute-start | bytes 4718600 | tf_op jit(solution)/shard_map/ppermute | solution.py:121
  13.4 93.2 %collective-permute-start.11 = (f32[288,1024]{1,0:T(8,128)}, f32[288,1024]{1,0:T(8,128)}, u32[]{:S(2)}, u32[]{:S(2)}) collective-permute-start(f32[288,1024]{1,0:T(8,128)} %slice.79), channel_id=1, source_target_pairs={{0,8},{4,28},{8,16},{12,4},{16,24},{20,12},{24,0},{28,20},{1,9},{5... | collective-permute-start | bytes 3538952 | tf_op jit(solution)/shard_map/ppermute | solution.py:121
  18.0 5.3 %copy-start.9 = (f32[1,3,2,192,192]{4,3,2,1,0:T(8,128)S(1)}, f32[1,3,2,192,192]{4,3,2,1,0:T(8,128)}, u32[]{:S(2)}) copy-start(f32[1,3,2,192,192]{4,3,2,1,0:T(8,128)} %param.10) | copy-start | bytes 2654212
  18.1 5.8 %copy-start.3 = (f32[768,1024]{1,0:T(8,128)S(1)}, f32[768,1024]{1,0:T(8,128)}, u32[]{:S(2)}) copy-start(f32[768,1024]{1,0:T(8,128)} %from_ref.1) | copy-start | bytes 9437188
  22.3 8.7 %copy-start.6 = (f32[768,768]{1,0:T(8,128)}, f32[768,768]{1,0:T(8,128)S(1)}, u32[]{:S(2)}) copy-start(f32[768,768]{1,0:T(8,128)S(1)} %get-tuple-element.10) | copy-start | bytes 7077892
  89.9 19.2 %collective-permute-start.1 = (f32[192,1024]{1,0:T(8,128)S(1)}, f32[192,1024]{1,0:T(8,128)}, u32[]{:S(2)}, u32[]{:S(2)}) collective-permute-start(f32[192,1024]{1,0:T(8,128)S(1)} %bitcast.57), channel_id=1, source_target_pairs={{0,8},{4,12},{8,0},{12,4},{16,24},{20,28},{24,16},{28,20},{1,9},{5... | collective-permute-start | bytes 2359304 | tf_op jit(solution)/shard_map/ppermute | solution.py:18
  94.3 10.8 %copy-start.5 = (f32[768,768]{1,0:T(8,128)S(1)}, f32[768,768]{1,0:T(8,128)}, u32[]{:S(2)}) copy-start(f32[768,768]{1,0:T(8,128)} %get-tuple-element.9) | copy-start | bytes 7077892
  94.3 10.0 %collective-permute-start.10 = (f32[96,1024]{1,0:T(8,128)}, f32[96,1024]{1,0:T(8,128)S(1)}, u32[]{:S(2)}, u32[]{:S(2)}) collective-permute-start(f32[96,1024]{1,0:T(8,128)} %collective-permute-done.5), channel_id=1, source_target_pairs={{0,4},{4,0},{8,12},{12,8},{16,20},{20,16},{24,28},{28,24},{1,5},{5... | collective-permute-start | bytes 1179656 | tf_op jit(solution)/shard_map/ppermute | solution.py:18
  104.3 77.0 %collective-permute-start.6 = (f32[384,1024]{1,0:T(8,128)S(1)}, f32[384,1024]{1,0:T(8,128)S(1)}, u32[]{:S(2)}, u32[]{:S(2)}) collective-permute-start(f32[384,1024]{1,0:T(8,128)S(1)} %shard_map.64), channel_id=1, source_target_pairs={{8,16},{20,12},{9,17},{21,13},{10,18},{22,14},{11,19},{23,15}} | collective-permute-start | bytes 4718600 | tf_op jit(solution)/shard_map/ppermute | solution.py:121
  105.0 9.7 %copy-start.7 = (f32[768,768]{1,0:T(8,128)S(1)}, f32[768,768]{1,0:T(8,128)}, u32[]{:S(2)}) copy-start(f32[768,768]{1,0:T(8,128)} %copy-done.6) | copy-start | bytes 7077892
  105.1 76.3 %slice-start = ((s8[7077888]{0:T(1024)(128)(4,1)}), s8[4194304]{0:T(1024)(128)(4,1)S(1)}, s32[]{:S(2)}) async-start(s8[7077888]{0:T(1024)(128)(4,1)} %bitcast.55), calls=%async_computation | async-start | bytes 8388608
  106.6 30.0 %collective-permute-start.4 = (f32[288,1024]{1,0:T(8,128)}, f32[288,1024]{1,0:T(8,128)}, u32[]{:S(2)}, u32[]{:S(2)}) collective-permute-start(f32[288,1024]{1,0:T(8,128)} %slice.79), channel_id=1, source_target_pairs={{0,24},{4,12},{8,0},{12,20},{16,8},{20,28},{24,16},{28,4},{1,25},{... | collective-permute-start | bytes 3538952 | tf_op jit(solution)/shard_map/ppermute | solution.py:121
  109.1 79.8 %collective-permute-start.7 = (f32[384,1024]{1,0:T(8,128)S(1)}, f32[384,1024]{1,0:T(8,128)S(1)}, u32[]{:S(2)}, u32[]{:S(2)}) collective-permute-start(f32[384,1024]{1,0:T(8,128)S(1)} %shard_map.64), channel_id=1, source_target_pairs={{0,8},{4,28},{12,4},{16,24},{24,0},{28,20},{1,9},{5,29},{13,5},{17... | collective-permute-start | bytes 4718600 | tf_op jit(solution)/shard_map/ppermute | solution.py:121
  114.7 5.8 %copy-start.4 = (f32[768,1024]{1,0:T(8,128)S(1)}, f32[768,1024]{1,0:T(8,128)}, u32[]{:S(2)}) copy-start(f32[768,1024]{1,0:T(8,128)} %fusion.14) | copy-start | bytes 9437188
  114.7 66.7 %slice-start.1 = ((s8[7077888]{0:T(1024)(128)(4,1)}), s8[2883584]{0:T(1024)(128)(4,1)S(1)}, s32[]{:S(2)}) async-start(s8[7077888]{0:T(1024)(128)(4,1)} %bitcast.55), calls=%async_computation.1 | async-start | bytes 5767168
  136.6 57.0 %collective-permute-start.12 = (f32[192,1024]{1,0:T(8,128)S(1)}, f32[192,1024]{1,0:T(8,128)S(1)}, u32[]{:S(2)}, u32[]{:S(2)}) collective-permute-start(f32[192,1024]{1,0:T(8,128)S(1)} %bitcast.58), channel_id=1, source_target_pairs={{0,16},{4,20},{24,8},{28,12},{1,17},{5,21},{25,9},{29,13},{2,18},{... | collective-permute-start | bytes 2359304 | tf_op jit(solution)/shard_map/ppermute | solution.py:18
  180.0 32.1 %collective-permute-start.13 = (f32[192,1024]{1,0:T(8,128)S(1)}, f32[192,1024]{1,0:T(8,128)S(1)}, u32[]{:S(2)}, u32[]{:S(2)}) collective-permute-start(f32[192,1024]{1,0:T(8,128)S(1)} %bitcast.59), channel_id=1, source_target_pairs={{8,24},{12,28},{16,0},{20,4},{9,25},{13,29},{17,1},{21,5},{10,26},... | collective-permute-start | bytes 2359304 | tf_op jit(solution)/shard_map/ppermute | solution.py:18
  181.3 40.3 %collective-permute-start.8 = (f32[384,1024]{1,0:T(8,128)}, f32[384,1024]{1,0:T(8,128)}, u32[]{:S(2)}, u32[]{:S(2)}) collective-permute-start(f32[384,1024]{1,0:T(8,128)} %collective-permute-done.3), channel_id=1, source_target_pairs={{0,4},{4,0},{8,12},{12,8},{16,20},{20,16},{24,28},{28,24},{1,5},{5... | collective-permute-start | bytes 4718600 | tf_op jit(solution)/shard_map/ppermute | solution.py:18
  188.9 32.7 %collective-permute-start.9 = (f32[288,1024]{1,0:T(8,128)}, f32[288,1024]{1,0:T(8,128)S(1)}, u32[]{:S(2)}, u32[]{:S(2)}) collective-permute-start(f32[288,1024]{1,0:T(8,128)} %collective-permute-done.4), channel_id=1, source_target_pairs={{0,4},{4,0},{8,12},{12,8},{16,20},{20,16},{24,28},{28,24},{1,5},{5... | collective-permute-start | bytes 3538952 | tf_op jit(solution)/shard_map/ppermute | solution.py:18
  193.6 36.4 %collective-permute-start.14 = (f32[96,1024]{1,0:T(8,128)}, f32[96,1024]{1,0:T(8,128)S(1)}, u32[]{:S(2)}, u32[]{:S(2)}) collective-permute-start(f32[96,1024]{1,0:T(8,128)} %slice.80), channel_id=1, source_target_pairs={{0,8},{4,28},{8,16},{12,4},{16,24},{20,12},{24,0},{28,20},{1,9},{5... | collective-permute-start | bytes 1179656 | tf_op jit(solution)/shard_map/ppermute | solution.py:121
  213.6 6.1 %copy-start.8 = (f32[768,1024]{1,0:T(8,128)S(1)}, f32[768,1024]{1,0:T(8,128)}, u32[]{:S(2)}) copy-start(f32[768,1024]{1,0:T(8,128)} %fusion) | copy-start | bytes 9437188
  229.0 3.3 %copy-start.1 = (f32[1,768,192]{1,2,0:T(8,128)S(1)}, f32[1,768,192]{1,2,0:T(8,128)}, u32[]{:S(2)}) copy-start(f32[1,768,192]{1,2,0:T(8,128)} %param.11) | copy-start | bytes 1769476
